TPU v7x, 32 devices: a whole 2x2x4 slice. The times are simulated.
32 devices in a mesh: dp: 4 (over z), expert: 4 (over y, x), seq: 2 (over core).
Axes of the slice: x: 2, y: 2, z: 4, core: 2. Of those that a mesh axis runs over, the one named last changes fastest.
Arguments:
- tokens: bfloat16 [2, 16, 2, 640, 768], P(None, ('dp', 'expert'), 'seq'), may hold values from -6 to 6
- previous_gate: float32 [2, 16, 2, 640, 12], P(None, ('dp', 'expert'), 'seq'), may hold values from -3 to 3
- routes: int32 [2, 16, 2, 640, 2], P(None, ('dp', 'expert'), 'seq'), may hold values from 0 to 11, all different within a row; in each aligned block of 640 rows (0 to 639, 640 to 1279, ..., all dimensions but the last counted through in order) at most 160 rows name the same one
- prompt_choice: int32 [2, 16, 2, 1], P(None, ('dp', 'expert'), 'seq'), may hold values from 0 to 3, as said below
- attention_gain: bfloat16 [768], P('dp'), may hold values from 0.5 to 1.5
- query_weight: bfloat16 [768, 768], P('dp'), may hold values from -0.21875 to 0.21875
- key_weight: bfloat16 [768, 768], P('dp'), may hold values from -0.3125 to 0.3125
- value_weight: bfloat16 [768, 768], P('dp'), may hold values from -0.21875 to 0.21875
- output_weight: bfloat16 [768, 768], P('dp'), may hold values from -3 to 3
- feedforward_gain: bfloat16 [768], P('dp'), may hold values from 0.5 to 1.5
- router_weight: bfloat16 [768, 12], P('dp'), may hold values from -0.15625 to 0.15625
- constant_weight: bfloat16 [768, 4], P('dp'), may hold values from -0.21875 to 0.21875
- constant_vector: bfloat16 [2, 768], P(None, 'dp'), may hold values from -5 to 5
- expert_gate: bfloat16 [8, 768, 2048], P('expert', 'dp'), may hold values from -0.21875 to 0.21875
- expert_up: bfloat16 [8, 768, 2048], P('expert', 'dp'), may hold values from -0.21875 to 0.21875
- expert_down: bfloat16 [8, 2048, 768], P('expert', 'dp'), may hold values from -0.25 to 0.25
- cotangent: bfloat16 [2, 16, 2, 640, 768], P(None, ('dp', 'expert'), 'seq'), may hold values from -6 to 6
Outputs:
- mixed: bfloat16 [2, 16, 2, 640, 768], P(None, ('dp', 'expert'), 'seq')
- input_grad: float32 [2, 16, 2, 640, 768], P(None, ('dp', 'expert'), 'seq')
- attention_gain_grad: float32 [768], P('dp')
- query_weight_grad: float32 [768, 768], P('dp')
- key_weight_grad: float32 [768, 768], P('dp')
- value_weight_grad: float32 [768, 768], P('dp')
- output_weight_grad: float32 [768, 768], P('dp')
- feedforward_gain_grad: float32 [768], P('dp')
- router_weight_grad: float32 [768, 12], P('dp')
- constant_weight_grad: float32 [768, 4], P('dp')
- constant_vector_grad: float32 [2, 768], P(None, 'dp')
- expert_gate_grad: float32 [8, 768, 2048], P('expert', 'dp')
- expert_up_grad: float32 [8, 768, 2048], P('expert', 'dp')
- expert_down_grad: float32 [8, 2048, 768], P('expert', 'dp')
Inputs may be any that keep to these rules, and one draw needn't show every extreme that they name: `routes`: in each aligned block of 640 rows (one block of one micro-batch) no number is named by more than 160 rows, a bound that some block reaches; a row names two different numbers. `prompt_choice`: in every micro-batch and data group, each of the 4 prompts is chosen by exactly 2 continuations.
All inputs are finite; a program needn't handle non-finite values.
Results may differ from a plain program's by a relative error of at most 0.03.
Values may be sent and summed in bfloat16 or wider, within the bound.
No kernel may reach another device: no remote copies, remote signals or barrier semaphores. Data moves between devices by JAX's collectives and lax.ppermute only.
A program may use at most 272 MiB of HBM per device.

v0:
```python
import jax
import jax.numpy as jnp
from jax import lax
from jax.sharding import PartitionSpec as P

HEADS = 12
HEAD_DIM = 64
PROMPT = 1024
CONT_LEN = 128


precise = lax.Precision.HIGHEST
epsilon = 1e-06
negative = -1e30
scale_factor = 0.125


def shortened(shard):
    return jax.tree.map(lambda a: a.astype(jnp.bfloat16) if a.dtype == jnp.float32 else a, shard)


def rotate_half(tensor):
    middle = tensor.shape[-1] // 2
    return jnp.concatenate([-tensor[..., middle:], tensor[..., :middle]], axis=-1)


def rotary_tables(position, head_size):
    middle = head_size // 2
    inverse = 10000.0 ** (-jnp.arange(middle, dtype=jnp.float32) * 2.0 / head_size)
    angles = position[..., None] * inverse
    cosine_table = jnp.concatenate([jnp.cos(angles), jnp.cos(angles)], axis=-1)[..., None, :]
    sine_table = jnp.concatenate([jnp.sin(angles), jnp.sin(angles)], axis=-1)[..., None, :]
    return (cosine_table, sine_table)


def rope_apply(tensor, cosine_table, sine_table):
    return tensor * cosine_table + rotate_half(tensor) * sine_table


def rope_back(tensor, cosine_table, sine_table):
    return tensor * cosine_table - rotate_half(tensor) * sine_table


def normalize(inputs):
    inverse = lax.rsqrt(jnp.mean(inputs * inputs, axis=-1, keepdims=True) + epsilon)
    return (inputs * inverse, inverse)


def norm_back(gradient, scaled, inverse):
    return inverse * (gradient - scaled * jnp.mean(gradient * scaled, axis=-1, keepdims=True))


def attend_scores(queries, key_rows, visible):
    scores = (
        jnp.einsum("bqhd,bkhd->bhqk", queries, key_rows, preferred_element_type=jnp.float32)
        * scale_factor
    )
    return jnp.where(visible, scores, negative)


def attend_forward(queries, key_rows, value_rows, visible):
    scores = attend_scores(queries, key_rows, visible)
    row_max = jnp.max(scores, axis=-1, keepdims=True)
    log_total = row_max + jnp.log(jnp.sum(jnp.exp(scores - row_max), axis=-1, keepdims=True))
    probabilities = jnp.exp(scores - log_total).astype(jnp.bfloat16)
    outputs = jnp.einsum(
        "bhqk,bkhd->bqhd", probabilities, value_rows, preferred_element_type=jnp.float32
    )
    return (outputs, log_total)


def attend_backward(queries, key_rows, value_rows, visible, log_total, grad_out, delta_sum):
    softmax_rows = jnp.exp(attend_scores(queries, key_rows, visible) - log_total)
    probabilities = softmax_rows.astype(jnp.bfloat16)
    grad_values = jnp.einsum(
        "bhqk,bqhd->bkhd", probabilities, grad_out, preferred_element_type=jnp.float32
    )
    grad_probs = jnp.einsum(
        "bqhd,bkhd->bhqk", grad_out, value_rows, preferred_element_type=jnp.float32
    )
    if delta_sum is None:
        delta_sum = jnp.sum(grad_probs * softmax_rows, axis=-1, keepdims=True)
    grad_scores = (softmax_rows * (grad_probs - delta_sum)).astype(jnp.bfloat16)
    grad_queries = (
        jnp.einsum("bhqk,bkhd->bqhd", grad_scores, key_rows, preferred_element_type=jnp.float32)
        * scale_factor
    )
    grad_keys = (
        jnp.einsum("bhqk,bqhd->bkhd", grad_scores, queries, preferred_element_type=jnp.float32)
        * scale_factor
    )
    return (grad_queries, grad_keys, grad_values)


def shared_forward(queries, key_rows, value_rows):
    scores = (
        jnp.einsum("bqhd,khd->bhqk", queries, key_rows, preferred_element_type=jnp.float32)
        * scale_factor
    )
    row_max = jnp.max(scores, axis=-1, keepdims=True)
    log_total = row_max + jnp.log(jnp.sum(jnp.exp(scores - row_max), axis=-1, keepdims=True))
    probabilities = jnp.exp(scores - log_total).astype(jnp.bfloat16)
    outputs = jnp.einsum(
        "bhqk,khd->bqhd", probabilities, value_rows, preferred_element_type=jnp.float32
    )
    return (outputs, log_total)


def shared_backward(queries, key_rows, value_rows, log_total, grad_out, delta_sum):
    scores = (
        jnp.einsum("bqhd,khd->bhqk", queries, key_rows, preferred_element_type=jnp.float32)
        * scale_factor
    )
    softmax_rows = jnp.exp(scores - log_total)
    probabilities = softmax_rows.astype(jnp.bfloat16)
    grad_values = jnp.einsum(
        "bhqk,bqhd->khd", probabilities, grad_out, preferred_element_type=jnp.float32
    )
    grad_probs = jnp.einsum(
        "bqhd,khd->bhqk", grad_out, value_rows, preferred_element_type=jnp.float32
    )
    grad_scores = (softmax_rows * (grad_probs - delta_sum)).astype(jnp.bfloat16)
    grad_queries = (
        jnp.einsum("bhqk,khd->bqhd", grad_scores, key_rows, preferred_element_type=jnp.float32)
        * scale_factor
    )
    grad_keys = (
        jnp.einsum("bhqk,bqhd->khd", grad_scores, queries, preferred_element_type=jnp.float32)
        * scale_factor
    )
    return (grad_queries, grad_keys, grad_values)


def slot_index(route_rows, route_count):
    flattened = route_rows.reshape(-1)
    one_hot = (flattened[:, None] == jnp.arange(route_count, dtype=jnp.int32)[None, :]).astype(
        jnp.int32
    )
    before = jnp.cumsum(one_hot, axis=0, dtype=jnp.int32) - one_hot
    return jnp.sum(before * one_hot, axis=1).reshape(route_rows.shape)


def per_device(
    tokens,
    previous_gate,
    routes,
    prompt_choice,
    attention_gain,
    query_weight,
    key_weight,
    value_weight,
    output_weight,
    feedforward_gain,
    router_weight,
    constant_weight,
    constant_vector,
    expert_gate,
    expert_up,
    expert_down,
    cotangent,
):
    micro_count = tokens.shape[0]
    row_count = tokens.shape[3]
    model_width = tokens.shape[4]
    head_count = HEADS
    head_size = HEAD_DIM
    cont_count = prompt_choice.shape[3]
    prompt_count = lax.axis_size("expert")
    half_count = lax.axis_size("seq")
    slot_count = prompt_count * half_count
    prompt_rows = PROMPT // half_count
    capacity = row_count // 4
    local_experts = expert_gate.shape[0]
    all_experts = local_experts * prompt_count
    route_count = all_experts + 4
    seq_index = lax.axis_index("seq")
    row_ids = jnp.arange(row_count, dtype=jnp.int32)
    position = jnp.where(
        row_ids < prompt_rows,
        seq_index * prompt_rows + row_ids,
        PROMPT + (row_ids - prompt_rows) % CONT_LEN,
    ).astype(jnp.float32)
    cosine_table, sine_table = rotary_tables(position, head_size)
    query_pos = seq_index * prompt_rows + jnp.arange(prompt_rows, dtype=jnp.int32)
    prompt_visible = (jnp.arange(PROMPT, dtype=jnp.int32)[None, :] <= query_pos[:, None])[
        None, None
    ]
    cont_rows = jnp.arange(CONT_LEN, dtype=jnp.int32)
    self_visible = (cont_rows[None, :] <= cont_rows[:, None])[None, None]
    prompt_ids = jnp.arange(prompt_count, dtype=jnp.int32)
    batch_ship = slot_count * cont_count
    live_count = half_count * cont_count
    mixed_parts = []
    input_parts = []
    totals = None
    for micro_index in range(micro_count):
        fetched = (
            lax.all_gather(attention_gain, "dp", axis=0, tiled=True),
            lax.all_gather(query_weight, "dp", axis=0, tiled=True),
            lax.all_gather(key_weight, "dp", axis=0, tiled=True),
            lax.all_gather(value_weight, "dp", axis=0, tiled=True),
            lax.all_gather(output_weight, "dp", axis=0, tiled=True),
            lax.all_gather(feedforward_gain, "dp", axis=0, tiled=True),
            lax.all_gather(router_weight, "dp", axis=0, tiled=True),
            lax.all_gather(constant_weight, "dp", axis=0, tiled=True),
            lax.all_gather(constant_vector, "dp", axis=1, tiled=True),
            lax.all_gather(expert_gate, "dp", axis=1, tiled=True),
            lax.all_gather(expert_up, "dp", axis=1, tiled=True),
            lax.all_gather(expert_down, "dp", axis=1, tiled=True),
        )
        (
            gain_attn,
            weight_query,
            weight_key,
            weight_value,
            weight_out,
            gain_ffn,
            weight_router,
            weight_const,
            vector_const,
            weight_gate,
            weight_up,
            weight_down,
        ) = fetched
        inputs = tokens[micro_index, 0, 0].astype(jnp.float32)
        scaled_attn, inverse_attn = normalize(inputs)
        attn_in = (scaled_attn * gain_attn.astype(jnp.float32)).astype(jnp.bfloat16)
        queries = rope_apply(
            jnp.dot(attn_in, weight_query, preferred_element_type=jnp.float32).reshape(
                row_count, head_count, head_size
            ),
            cosine_table,
            sine_table,
        ).astype(jnp.bfloat16)
        key_rows = rope_apply(
            jnp.dot(attn_in, weight_key, preferred_element_type=jnp.float32).reshape(
                row_count, head_count, head_size
            ),
            cosine_table,
            sine_table,
        ).astype(jnp.bfloat16)
        value_rows = (
            jnp.dot(attn_in, weight_value, preferred_element_type=jnp.float32)
            .astype(jnp.bfloat16)
            .reshape(row_count, head_count, head_size)
        )
        local_keys = key_rows[:prompt_rows]
        local_values = value_rows[:prompt_rows]
        half_keys, half_values = (
            lax.all_gather(local_keys.reshape(prompt_rows, model_width), "seq", axis=0, tiled=True),
            lax.all_gather(
                local_values.reshape(prompt_rows, model_width), "seq", axis=0, tiled=True
            ),
        )
        own_keys = half_keys.reshape(1, PROMPT, head_count, head_size)
        own_values = half_values.reshape(1, PROMPT, head_count, head_size)
        prompt_out, prompt_total = attend_forward(
            queries[None, :prompt_rows], own_keys, own_values, prompt_visible
        )
        chosen = prompt_choice[micro_index, 0, 0]
        choice_marks = (chosen[:, None] == prompt_ids[None, :]).astype(jnp.float32)
        slot_marks = jnp.repeat(choice_marks, half_count, axis=1).T
        cont_queries = queries[prompt_rows:].reshape(cont_count, CONT_LEN, head_count, head_size)
        ship_queries = jnp.where(
            slot_marks[:, :, None, None] > 0.5,
            cont_queries.reshape(cont_count, CONT_LEN, model_width)[None],
            jnp.zeros((), jnp.bfloat16),
        )
        ship_flags = slot_marks.astype(jnp.bfloat16)
        arrived_raw, arrived_flags = (
            lax.all_to_all(
                ship_queries, ("expert", "seq"), split_axis=0, concat_axis=0, tiled=True
            ),
            lax.all_to_all(ship_flags, ("expert", "seq"), split_axis=0, concat_axis=0, tiled=True),
        )
        arrived_queries = arrived_raw.reshape(batch_ship, CONT_LEN, head_count, head_size)
        live_rank = jnp.where(arrived_flags.reshape(batch_ship) > 0.5, 0, 1).astype(
            jnp.int32
        ) * batch_ship + jnp.arange(batch_ship, dtype=jnp.int32)
        live_slots = jnp.argsort(live_rank)[:live_count]
        live_queries = jnp.take(arrived_queries, live_slots, axis=0)
        part_out, part_total = shared_forward(live_queries, local_keys, local_values)
        full_out = (
            jnp.zeros((batch_ship, CONT_LEN, model_width), jnp.float32)
            .at[live_slots]
            .set(part_out.reshape(live_count, CONT_LEN, model_width))
        )
        full_total = (
            jnp.zeros((batch_ship, head_count, CONT_LEN), jnp.float32)
            .at[live_slots]
            .set(part_total.reshape(live_count, head_count, CONT_LEN))
        )
        back_out, back_total = (
            lax.all_to_all(
                full_out.reshape(slot_count, cont_count, CONT_LEN, model_width).astype(
                    jnp.bfloat16
                ),
                ("expert", "seq"),
                split_axis=0,
                concat_axis=0,
                tiled=True,
            ).astype(jnp.float32),
            lax.all_to_all(
                full_total.reshape(slot_count, cont_count, head_count, CONT_LEN).astype(
                    jnp.bfloat16
                ),
                ("expert", "seq"),
                split_axis=0,
                concat_axis=0,
                tiled=True,
            ).astype(jnp.float32),
        )
        picked_out = jnp.einsum(
            "ce,esclw->sclw",
            choice_marks,
            back_out.reshape(prompt_count, half_count, cont_count, CONT_LEN, model_width),
            precision=precise,
        )
        picked_total = jnp.einsum(
            "ce,eschq->schq",
            choice_marks,
            back_total.reshape(prompt_count, half_count, cont_count, head_count, CONT_LEN),
            precision=precise,
        )
        self_keys = key_rows[prompt_rows:].reshape(cont_count, CONT_LEN, head_count, head_size)
        self_values = value_rows[prompt_rows:].reshape(cont_count, CONT_LEN, head_count, head_size)
        self_out, self_total = attend_forward(cont_queries, self_keys, self_values, self_visible)
        total_stack = jnp.concatenate([self_total[None, ..., 0], picked_total], axis=0)
        stack_top = jnp.max(total_stack, axis=0)
        cont_total = stack_top + jnp.log(jnp.sum(jnp.exp(total_stack - stack_top), axis=0))
        factors = jnp.exp(total_stack - cont_total).transpose(0, 1, 3, 2)[..., None]
        out_stack = jnp.concatenate(
            [
                self_out[None],
                picked_out.reshape(half_count, cont_count, CONT_LEN, head_count, head_size),
            ],
            axis=0,
        )
        cont_out = jnp.sum(factors * out_stack, axis=0)
        attn_low = jnp.concatenate(
            [
                prompt_out.reshape(prompt_rows, model_width),
                cont_out.reshape(cont_count * CONT_LEN, model_width),
            ],
            axis=0,
        ).astype(jnp.bfloat16)
        hidden_state = inputs + jnp.dot(attn_low, weight_out, preferred_element_type=jnp.float32)
        scaled_ffn, inverse_ffn = normalize(hidden_state)
        normed = scaled_ffn * gain_ffn.astype(jnp.float32)
        normed_low = normed.astype(jnp.bfloat16)
        route_rows = routes[micro_index, 0, 0]
        route_marks = (route_rows[:, :, None] == jnp.arange(route_count, dtype=jnp.int32)).astype(
            jnp.float32
        )
        logits = (
            jnp.dot(normed_low, weight_router, preferred_element_type=jnp.float32)
            + previous_gate[micro_index, 0, 0]
        )
        chosen_logits = jnp.sum(logits[:, None, :] * route_marks, axis=-1)
        gate_max = jnp.max(chosen_logits, axis=-1, keepdims=True)
        gate_exp = jnp.exp(chosen_logits - gate_max)
        gate_weights = gate_exp / jnp.sum(gate_exp, axis=-1, keepdims=True)
        slot_rows = slot_index(route_rows, route_count)
        is_ffn = route_rows < all_experts
        ffn_mask = is_ffn.astype(jnp.float32)
        buffer_index = (jnp.minimum(route_rows, all_experts - 1) * capacity + slot_rows).reshape(-1)
        send_index = jnp.where(is_ffn.reshape(-1), buffer_index, all_experts * capacity)
        rows_twice = jnp.broadcast_to(normed_low[:, None, :], (row_count, 2, model_width)).reshape(
            row_count * 2, model_width
        )
        outgoing = (
            jnp.zeros((all_experts * capacity, model_width), jnp.bfloat16)
            .at[send_index]
            .set(rows_twice, mode="drop")
            .reshape(prompt_count, local_experts, capacity, model_width)
        )
        arrived_rows = lax.all_to_all(outgoing, "expert", split_axis=0, concat_axis=0, tiled=True)
        gate_rows = jnp.einsum(
            "sebd,edf->sebf", arrived_rows, weight_gate, preferred_element_type=jnp.float32
        )
        up_rows = jnp.einsum(
            "sebd,edf->sebf", arrived_rows, weight_up, preferred_element_type=jnp.float32
        )
        hidden_rows = (gate_rows * jax.nn.sigmoid(gate_rows) * up_rows).astype(jnp.bfloat16)
        result = jnp.einsum(
            "sebf,efd->sebd", hidden_rows, weight_down, preferred_element_type=jnp.float32
        ).astype(jnp.bfloat16)
        returned = lax.all_to_all(
            result, "expert", split_axis=0, concat_axis=0, tiled=True
        ).reshape(all_experts * capacity, model_width)
        ffn_rows = (
            jnp.take(returned, buffer_index, axis=0)
            .reshape(row_count, 2, model_width)
            .astype(jnp.float32)
            * ffn_mask[:, :, None]
        )
        const_logits = jnp.dot(
            normed_low, weight_const, preferred_element_type=jnp.float32
        ).reshape(row_count, 2, 2)
        const_exp = jnp.exp(const_logits - jnp.max(const_logits, axis=-1, keepdims=True))
        alphas = const_exp / jnp.sum(const_exp, axis=-1, keepdims=True)
        vector_full = vector_const.astype(jnp.float32)
        const_out = alphas[:, :, 0:1] * normed[:, None, :] + alphas[:, :, 1:2] * vector_full[None]
        copy_mask = (route_rows == all_experts + 1).astype(jnp.float32)
        const_mask = route_marks[:, :, all_experts + 2 :]
        branches = (
            ffn_rows
            + copy_mask[:, :, None] * normed[:, None, :]
            + const_mask[:, :, 0:1] * const_out[:, None, 0]
            + const_mask[:, :, 1:2] * const_out[:, None, 1]
        )
        mixed_rows = hidden_state + jnp.sum(gate_weights[:, :, None] * branches, axis=1)
        mixed_parts.append(mixed_rows.astype(jnp.bfloat16))
        grad_mixed = cotangent[micro_index, 0, 0].astype(jnp.float32)
        grad_gates = jnp.sum(grad_mixed[:, None, :] * branches, axis=-1)
        grad_branch = gate_weights[:, :, None] * grad_mixed[:, None, :]
        grad_send = (
            jnp.zeros((all_experts * capacity, model_width), jnp.bfloat16)
            .at[send_index]
            .set(grad_branch.astype(jnp.bfloat16).reshape(row_count * 2, model_width), mode="drop")
            .reshape(prompt_count, local_experts, capacity, model_width)
        )
        grad_result = lax.all_to_all(grad_send, "expert", split_axis=0, concat_axis=0, tiled=True)
        sigmoid_gate = jax.nn.sigmoid(gate_rows)
        activated = gate_rows * sigmoid_gate
        hidden_low = (activated * up_rows).astype(jnp.bfloat16)
        grad_down = jnp.einsum(
            "sebf,sebd->efd", hidden_low, grad_result, preferred_element_type=jnp.float32
        )
        grad_hidden = jnp.einsum(
            "sebd,efd->sebf", grad_result, weight_down, preferred_element_type=jnp.float32
        )
        grad_up_pre = (grad_hidden * activated).astype(jnp.bfloat16)
        grad_gate_pre = (
            grad_hidden * up_rows * sigmoid_gate * (1.0 + gate_rows * (1.0 - sigmoid_gate))
        ).astype(jnp.bfloat16)
        grad_gate = jnp.einsum(
            "sebd,sebf->edf", arrived_rows, grad_gate_pre, preferred_element_type=jnp.float32
        )
        grad_up = jnp.einsum(
            "sebd,sebf->edf", arrived_rows, grad_up_pre, preferred_element_type=jnp.float32
        )
        grad_arrived = (
            jnp.einsum(
                "sebf,edf->sebd", grad_gate_pre, weight_gate, preferred_element_type=jnp.float32
            )
            + jnp.einsum(
                "sebf,edf->sebd", grad_up_pre, weight_up, preferred_element_type=jnp.float32
            )
        ).astype(jnp.bfloat16)
        grad_returned = lax.all_to_all(
            grad_arrived, "expert", split_axis=0, concat_axis=0, tiled=True
        ).reshape(all_experts * capacity, model_width)
        grad_normed = jnp.sum(
            jnp.take(grad_returned, buffer_index, axis=0)
            .reshape(row_count, 2, model_width)
            .astype(jnp.float32)
            * ffn_mask[:, :, None],
            axis=1,
        )
        grad_normed = grad_normed + jnp.sum(copy_mask[:, :, None] * grad_branch, axis=1)
        grad_const = jnp.sum(const_mask[:, :, :, None] * grad_branch[:, :, None, :], axis=1)
        grad_normed = grad_normed + jnp.sum(alphas[:, :, 0:1] * grad_const, axis=1)
        grad_alphas = jnp.stack(
            [
                jnp.sum(grad_const * normed[:, None, :], axis=-1),
                jnp.sum(grad_const * vector_full[None], axis=-1),
            ],
            axis=-1,
        )
        grad_vector = jnp.sum(alphas[:, :, 1:2] * grad_const, axis=0)
        grad_const_logits = (
            alphas * (grad_alphas - jnp.sum(alphas * grad_alphas, axis=-1, keepdims=True))
        ).reshape(row_count, 4)
        grad_chosen = gate_weights * (
            grad_gates - jnp.sum(gate_weights * grad_gates, axis=-1, keepdims=True)
        )
        grad_logits = jnp.sum(grad_chosen[:, :, None] * route_marks, axis=1)
        grad_small = jnp.concatenate([grad_logits, grad_const_logits], axis=1)
        small_weights = jnp.concatenate([weight_router, weight_const], axis=1).astype(jnp.float32)
        grad_small_weights = jnp.dot(
            normed_low.astype(jnp.float32).T, grad_small, precision=precise
        )
        grad_normed = grad_normed + jnp.dot(grad_small, small_weights.T, precision=precise)
        grad_gain_ffn = jnp.sum(grad_normed * scaled_ffn, axis=0)
        grad_state = grad_mixed + norm_back(
            grad_normed * gain_ffn.astype(jnp.float32), scaled_ffn, inverse_ffn
        )
        grad_state_low = grad_state.astype(jnp.bfloat16)
        grad_output = jnp.einsum(
            "rd,re->de", attn_low, grad_state_low, preferred_element_type=jnp.float32
        )
        grad_attn = (
            jnp.einsum("re,de->rd", grad_state_low, weight_out, preferred_element_type=jnp.float32)
            .astype(jnp.bfloat16)
            .reshape(row_count, head_count, head_size)
        )
        grad_prompt_q, grad_prompt_k, grad_prompt_v = attend_backward(
            queries[None, :prompt_rows],
            own_keys,
            own_values,
            prompt_visible,
            prompt_total,
            grad_attn[None, :prompt_rows],
            None,
        )
        grad_cont = grad_attn[prompt_rows:].reshape(cont_count, CONT_LEN, head_count, head_size)
        cont_delta = jnp.sum(grad_cont.astype(jnp.float32) * cont_out, axis=-1).transpose(0, 2, 1)
        grad_self_q, grad_self_k, grad_self_v = attend_backward(
            cont_queries,
            self_keys,
            self_values,
            self_visible,
            cont_total[..., None],
            grad_cont,
            cont_delta[..., None],
        )
        live = slot_marks[:, :, None, None] > 0.5
        ship_grad = jnp.where(
            live,
            grad_cont.reshape(cont_count, CONT_LEN, model_width).astype(jnp.float32)[None],
            0.0,
        )
        ship_total = jnp.broadcast_to(
            cont_total[None], (slot_count, cont_count, head_count, CONT_LEN)
        )
        ship_delta = jnp.where(live, cont_delta[None], 0.0)
        got_grad, got_total, got_delta = (
            lax.all_to_all(
                ship_grad.astype(jnp.bfloat16),
                ("expert", "seq"),
                split_axis=0,
                concat_axis=0,
                tiled=True,
            ).astype(ship_grad.dtype),
            lax.all_to_all(
                shortened(ship_total), ("expert", "seq"), split_axis=0, concat_axis=0, tiled=True
            ).astype(ship_total.dtype),
            lax.all_to_all(
                shortened(ship_delta), ("expert", "seq"), split_axis=0, concat_axis=0, tiled=True
            ).astype(ship_delta.dtype),
        )
        live_grad = jnp.take(
            got_grad.reshape(batch_ship, CONT_LEN, head_count, head_size), live_slots, axis=0
        ).astype(jnp.bfloat16)
        live_total = jnp.take(
            got_total.reshape(batch_ship, head_count, CONT_LEN), live_slots, axis=0
        )[..., None]
        live_delta = jnp.take(
            got_delta.reshape(batch_ship, head_count, CONT_LEN), live_slots, axis=0
        )[..., None]
        part_q, part_k, part_v = shared_backward(
            live_queries, local_keys, local_values, live_total, live_grad, live_delta
        )
        full_q = (
            jnp.zeros((batch_ship, CONT_LEN, model_width), jnp.float32)
            .at[live_slots]
            .set(part_q.reshape(live_count, CONT_LEN, model_width))
        )
        back_q = lax.all_to_all(
            full_q.reshape(slot_count, cont_count, CONT_LEN, model_width).astype(jnp.bfloat16),
            ("expert", "seq"),
            split_axis=0,
            concat_axis=0,
            tiled=True,
        ).astype(jnp.float32)
        remote_q = jnp.einsum(
            "ce,esclw->clw",
            choice_marks,
            back_q.reshape(prompt_count, half_count, cont_count, CONT_LEN, model_width),
            precision=precise,
        )
        mine_keys, mine_values = (
            lax.psum_scatter(
                grad_prompt_k.reshape(PROMPT, model_width).astype(jnp.bfloat16),
                "seq",
                scatter_dimension=0,
                tiled=True,
            ).astype(jnp.float32),
            lax.psum_scatter(
                grad_prompt_v.reshape(PROMPT, model_width).astype(jnp.bfloat16),
                "seq",
                scatter_dimension=0,
                tiled=True,
            ).astype(jnp.float32),
        )
        grad_keys_all = jnp.concatenate(
            [
                mine_keys + part_k.reshape(prompt_rows, model_width),
                grad_self_k.reshape(cont_count * CONT_LEN, model_width),
            ],
            axis=0,
        )
        grad_values_all = jnp.concatenate(
            [
                mine_values + part_v.reshape(prompt_rows, model_width),
                grad_self_v.reshape(cont_count * CONT_LEN, model_width),
            ],
            axis=0,
        )
        grad_queries_all = jnp.concatenate(
            [
                grad_prompt_q.reshape(prompt_rows, model_width),
                grad_self_q.reshape(cont_count * CONT_LEN, model_width)
                + remote_q.reshape(cont_count * CONT_LEN, model_width),
            ],
            axis=0,
        )
        grad_query_low = (
            rope_back(
                grad_queries_all.reshape(row_count, head_count, head_size), cosine_table, sine_table
            )
            .astype(jnp.bfloat16)
            .reshape(row_count, model_width)
        )
        grad_key_low = (
            rope_back(
                grad_keys_all.reshape(row_count, head_count, head_size), cosine_table, sine_table
            )
            .astype(jnp.bfloat16)
            .reshape(row_count, model_width)
        )
        grad_value_low = grad_values_all.astype(jnp.bfloat16)
        grad_query = jnp.einsum(
            "rd,re->de", attn_in, grad_query_low, preferred_element_type=jnp.float32
        )
        grad_key = jnp.einsum(
            "rd,re->de", attn_in, grad_key_low, preferred_element_type=jnp.float32
        )
        grad_value = jnp.einsum(
            "rd,re->de", attn_in, grad_value_low, preferred_element_type=jnp.float32
        )
        grad_attn_in = (
            jnp.einsum(
                "re,de->rd", grad_query_low, weight_query, preferred_element_type=jnp.float32
            )
            + jnp.einsum("re,de->rd", grad_key_low, weight_key, preferred_element_type=jnp.float32)
            + jnp.einsum(
                "re,de->rd", grad_value_low, weight_value, preferred_element_type=jnp.float32
            )
        )
        grad_gain_attn = jnp.sum(grad_attn_in * scaled_attn, axis=0)
        input_parts.append(
            grad_state
            + norm_back(grad_attn_in * gain_attn.astype(jnp.float32), scaled_attn, inverse_attn)
        )
        complete = (
            grad_gain_attn,
            grad_query,
            grad_key,
            grad_value,
            grad_output,
            grad_gain_ffn,
            grad_small_weights[:, :route_count],
            grad_small_weights[:, route_count:],
            grad_vector,
            grad_gate,
            grad_up,
            grad_down,
        )
        portion = (
            lax.psum_scatter(
                complete[0].astype(jnp.bfloat16), "dp", scatter_dimension=0, tiled=True
            ).astype(jnp.float32),
            lax.psum_scatter(
                complete[1].astype(jnp.bfloat16), "dp", scatter_dimension=0, tiled=True
            ).astype(jnp.float32),
            lax.psum_scatter(
                complete[2].astype(jnp.bfloat16), "dp", scatter_dimension=0, tiled=True
            ).astype(jnp.float32),
            lax.psum_scatter(
                complete[3].astype(jnp.bfloat16), "dp", scatter_dimension=0, tiled=True
            ).astype(jnp.float32),
            lax.psum_scatter(
                complete[4].astype(jnp.bfloat16), "dp", scatter_dimension=0, tiled=True
            ).astype(jnp.float32),
            lax.psum_scatter(
                complete[5].astype(jnp.bfloat16), "dp", scatter_dimension=0, tiled=True
            ).astype(jnp.float32),
            lax.psum_scatter(
                complete[6].astype(jnp.bfloat16), "dp", scatter_dimension=0, tiled=True
            ).astype(jnp.float32),
            lax.psum_scatter(
                complete[7].astype(jnp.bfloat16), "dp", scatter_dimension=0, tiled=True
            ).astype(jnp.float32),
            lax.psum_scatter(
                complete[8].astype(jnp.bfloat16), "dp", scatter_dimension=1, tiled=True
            ).astype(jnp.float32),
            lax.psum_scatter(
                complete[9].astype(jnp.bfloat16), "dp", scatter_dimension=1, tiled=True
            ).astype(jnp.float32),
            lax.psum_scatter(
                complete[10].astype(jnp.bfloat16), "dp", scatter_dimension=1, tiled=True
            ).astype(jnp.float32),
            lax.psum_scatter(
                complete[11].astype(jnp.bfloat16), "dp", scatter_dimension=1, tiled=True
            ).astype(jnp.float32),
        )
        totals = portion if totals is None else jax.tree.map(jnp.add, totals, portion)
    (
        sum_gain_attn,
        sum_query,
        sum_key,
        sum_value,
        sum_output,
        sum_gain_ffn,
        sum_router,
        sum_const,
        sum_vector,
        sum_gate,
        sum_up,
        sum_down,
    ) = totals
    dense_sums = (
        lax.psum(sum_gain_attn.astype(jnp.bfloat16), ("expert", "seq")).astype(jnp.float32),
        lax.psum(sum_query.astype(jnp.bfloat16), ("expert", "seq")).astype(jnp.float32),
        lax.psum(sum_key.astype(jnp.bfloat16), ("expert", "seq")).astype(jnp.float32),
        lax.psum(sum_value.astype(jnp.bfloat16), ("expert", "seq")).astype(jnp.float32),
        lax.psum(sum_output.astype(jnp.bfloat16), ("expert", "seq")).astype(jnp.float32),
        lax.psum(sum_gain_ffn.astype(jnp.bfloat16), ("expert", "seq")).astype(jnp.float32),
        lax.psum(sum_router.astype(jnp.bfloat16), ("expert", "seq")).astype(jnp.float32),
        lax.psum(sum_const.astype(jnp.bfloat16), ("expert", "seq")).astype(jnp.float32),
        lax.psum(sum_vector.astype(jnp.bfloat16), ("expert", "seq")).astype(jnp.float32),
    )
    expert_sums = (
        lax.psum(sum_gate.astype(jnp.bfloat16), "seq").astype(jnp.float32),
        lax.psum(sum_up.astype(jnp.bfloat16), "seq").astype(jnp.float32),
        lax.psum(sum_down.astype(jnp.bfloat16), "seq").astype(jnp.float32),
    )
    mixed_out = jnp.stack(mixed_parts).reshape(micro_count, 1, 1, row_count, model_width)
    input_out = jnp.stack(input_parts).reshape(micro_count, 1, 1, row_count, model_width)
    return (
        mixed_out,
        input_out,
        dense_sums[0],
        dense_sums[1],
        dense_sums[2],
        dense_sums[3],
        dense_sums[4],
        dense_sums[5],
        dense_sums[6],
        dense_sums[7],
        dense_sums[8],
        expert_sums[0],
        expert_sums[1],
        expert_sums[2],
    )


def solution(mesh):
    in_specs = (
        P(None, ("dp", "expert"), "seq", None, None),
        P(None, ("dp", "expert"), "seq", None, None),
        P(None, ("dp", "expert"), "seq", None, None),
        P(None, ("dp", "expert"), "seq", None),
        P("dp"),
        P("dp", None),
        P("dp", None),
        P("dp", None),
        P("dp", None),
        P("dp"),
        P("dp", None),
        P("dp", None),
        P(None, "dp"),
        P("expert", "dp", None),
        P("expert", "dp", None),
        P("expert", "dp", None),
        P(None, ("dp", "expert"), "seq", None, None),
    )
    out_specs = (
        P(None, ("dp", "expert"), "seq", None, None),
        P(None, ("dp", "expert"), "seq", None, None),
        P("dp"),
        P("dp", None),
        P("dp", None),
        P("dp", None),
        P("dp", None),
        P("dp"),
        P("dp", None),
        P("dp", None),
        P(None, "dp"),
        P("expert", "dp", None),
        P("expert", "dp", None),
        P("expert", "dp", None),
    )
    return jax.shard_map(
        per_device, mesh=mesh, in_specs=in_specs, out_specs=out_specs, check_vma=False
    )
```

profile of v0, /device:TPU:0, one launch (start us, length us, event | category | flops | bytes accessed | tf_op | source)
XLA Modules:
  0.0 2397.1 jit_solution(8335297911663503780)
XLA Ops:
  13.2 13.9 all-reduce.9
  45.2 28.5 %all-gather.19.cloned.1.call-done = bf16[768,768]{1,0:T(8,128)(2,1)} async-done(((bf16[192,768]{1,0:T(8,128)(2,1)}), bf16[768,768]{1,0:T(8,128)(2,1)}) %all-gather.19.cloned.1.call-update) | async-done | bytes 1179664 | tf_op jit(solution)/shard_map/all_gather | solution.py:199
  85.3 19.6 all-gather.15.cloned.1.call-done
  147.9 13.8 all-gather
  235.7 14.9 all-to-all-done.7
  426.7 80.9 %all-gather.31.cloned.1.call-done = bf16[2,2048,768]{2,1,0:T(8,128)(2,1)} async-done(((bf16[2,512,768]{2,1,0:T(8,128)(2,1)}), bf16[2,2048,768]{2,1,0:T(8,128)(2,1)}) %all-gather.31.cloned.1.call-update) | async-done | bytes 6291472 | tf_op jit(solution)/shard_map/all_gather | solution.py:209
  526.8 18.3 all-to-all-done.5
  601.6 14.9 scatter_custom_fusion.6
  645.7 15.4 fusion.12
  753.1 26.1 %multiply_reduce_fusion.1 = (f32[12,512]{1,0:T(8,128)S(1)}, f32[12,512]{1,0:T(8,128)S(1)}, f32[12,512,1024]{2,1,0:T(8,128)}) fusion(f32[12,512,1024]{2,1,0:T(8,128)} %get-tuple-element.317, f32[12,512]{1,0:T(8,128)S(1)} %copy-done.122, pred[512,1024]{1,0:T(8,128)(4,1)S(1)} %copy-done.4, f32[12,512,1024]{2,1,0:T(8,128)} %fusion.263, ...), kind=kOutput, calls=%fused_computation.27 | convolution fusion | flops 855625728 | bytes 78454784 | tf_op jit(solution)/shard_map/bqhd,bkhd->bhqk/dot_general | solution.py:78
  779.2 30.1 %multiply_convert_fusion.1 = (bf16[12,512,1024]{2,1,0:T(8,128)(2,1)}, f32[12,512]{1,0:T(8,128)S(1)}) fusion(f32[12,512,1024]{2,1,0:T(8,128)} %get-tuple-element.323, f32[12,512,1024]{2,1,0:T(8,128)} %get-tuple-element.317, f32[12,512]{1,0:T(8,128)S(1)} %get-tuple-element.156, f32[12,512]{1,0:T(8,128)S(1)} %copy-done.122, pred[512,1024]{1,0:T(8,128)(4,1)S(1)} %copy-done.4, ...), kind=kLoop, calls=%fused_computation.26 | loop fusion | flops 62908416 | bytes 88702976 | tf_op jit(solution)/shard_map/convert_element_type | solution.py:83
  955.3 14.9 scatter_custom_fusion.8
  974.9 12.8 convolution_convert_fusion.1
  997.3 15.3 fusion.8
  1101.4 13.0 convolution_convert_fusion
  1114.4 21.5 multiply_reduce_fusion
  1136.0 17.7 multiply_convert_fusion
  1462.3 27.6 %reduce-scatter.51.cloned.1.call-done = bf16[192,768]{1,0:T(8,128)(2,1)} async-done(((bf16[768,768]{1,0:T(8,128)(2,1)}), bf16[192,768]{1,0:T(8,128)(2,1)}) %reduce-scatter.51.cloned.1.call-update) | async-done | bytes 294928 | tf_op jit(solution)/shard_map/reduce_scatter | solution.py:668
  1492.1 109.4 %reduce-scatter.65.cloned.1.call-done = bf16[2,192,2048]{2,1,0:T(8,128)(2,1)} async-done(((bf16[2,768,2048]{2,1,0:T(8,128)(2,1)}), bf16[2,192,2048]{2,1,0:T(8,128)(2,1)}) %reduce-scatter.65.cloned.1.call-update) | async-done | bytes 1572880 | tf_op jit(solution)/shard_map/reduce_scatter | solution.py:692
  1601.5 113.6 %reduce-scatter.67.cloned.1.call-done = bf16[2,192,2048]{2,1,0:T(8,128)(2,1)} async-done(((bf16[2,768,2048]{2,1,0:T(8,128)(2,1)}), bf16[2,192,2048]{2,1,0:T(8,128)(2,1)}) %reduce-scatter.67.cloned.1.call-update) | async-done | bytes 1572880 | tf_op jit(solution)/shard_map/reduce_scatter | solution.py:692
  1718.9 109.7 %reduce-scatter.69.cloned.1.call-done = bf16[2,512,768]{2,1,0:T(8,128)(2,1)} async-done(((bf16[2,2048,768]{2,1,0:T(8,128)(2,1)}), bf16[2,512,768]{2,1,0:T(8,128)(2,1)}) %reduce-scatter.69.cloned.1.call-update) | async-done | bytes 1572880 | tf_op jit(solution)/shard_map/reduce_scatter | solution.py:695
  1828.6 113.5 %reduce-scatter.71.cloned.1.call-done = bf16[2,512,768]{2,1,0:T(8,128)(2,1)} async-done(((bf16[2,2048,768]{2,1,0:T(8,128)(2,1)}), bf16[2,512,768]{2,1,0:T(8,128)(2,1)}) %reduce-scatter.71.cloned.1.call-update) | async-done | bytes 1572880 | tf_op jit(solution)/shard_map/reduce_scatter | solution.py:695
  1945.4 110.2 %reduce-scatter.61.cloned.1.call-done = bf16[2,192,2048]{2,1,0:T(8,128)(2,1)} async-done(((bf16[2,768,2048]{2,1,0:T(8,128)(2,1)}), bf16[2,192,2048]{2,1,0:T(8,128)(2,1)}) %reduce-scatter.61.cloned.1.call-update) | async-done | bytes 1572880 | tf_op jit(solution)/shard_map/reduce_scatter | solution.py:689
  2055.7 113.6 %reduce-scatter.63.cloned.1.call-done = bf16[2,192,2048]{2,1,0:T(8,128)(2,1)} async-done(((bf16[2,768,2048]{2,1,0:T(8,128)(2,1)}), bf16[2,192,2048]{2,1,0:T(8,128)(2,1)}) %reduce-scatter.63.cloned.1.call-update) | async-done | bytes 1572880 | tf_op jit(solution)/shard_map/reduce_scatter | solution.py:689
  2173.7 17.9 reduce-scatter.81.cloned.1.call-done
  2192.4 19.3 reduce-scatter.77.cloned.1.call-done
  2212.5 19.3 reduce-scatter.73.cloned.1.call-done
  2235.6 16.1 reduce-scatter.83.cloned.1.call-done
  2254.4 17.4 reduce-scatter.79.cloned.1.call-done
  2273.3 18.6 reduce-scatter.75.cloned.1.call-done
  2318.3 22.5 all-reduce.6
  2356.9 25.6 %all-reduce.16.cloned.1.call-done = (bf16[2,192,2048]{2,1,0:T(8,128)(2,1)}, bf16[2,192,2048]{2,1,0:T(8,128)(2,1)}, bf16[2,512,768]{2,1,0:T(8,128)(2,1)}) async-done(((bf16[2,192,2048]{2,1,0:T(8,128)(2,1)}, bf16[2,192,2048]{2,1,0:T(8,128)(2,1)}, bf16[2,512,768]{2,1,0:T(8,128)(2,1)}), (bf16[2,192,2048]{2,1,0:T(8,128)(2,1)}, bf16[2,192,2048]{2,1,0:T(8,128)(2,1)}, ...) | async-done | bytes 4718608 | tf_op jit(solution)/shard_map/psum | solution.py:726
  (1165 shorter events, 1151.2 us)
Async XLA Ops:
  9.4 298.5 %all-gather.23.cloned.1.call-start = ((), (), s32[]{:S(2)}) async-start(), calls=%async_computation.52 | async-start | bytes 2359296 | tf_op jit(solution)/shard_map/all_gather | solution.py:250
  85.2 246.7 %all-gather.17.cloned.1.call-start = ((), (), s32[]{:S(2)}) async-start(), calls=%async_computation.49 | async-start | bytes 2359296 | tf_op jit(solution)/shard_map/all_gather | solution.py:251
  109.3 246.6 %all-gather.25.cloned.1.call-start = ((), (), s32[]{:S(2)}) async-start(), calls=%async_computation.53 | async-start | bytes 1474560 | tf_op jit(solution)/shard_map/all_gather | solution.py:202
  109.9 292.7 %all-gather.27.cloned.1.call-start = ((), (), s32[]{:S(2)}) async-start(), calls=%async_computation.54 | async-start | bytes 7864320 | tf_op jit(solution)/shard_map/all_gather | solution.py:207
  110.7 303.7 %all-gather.29.cloned.1.call-start = ((), (), s32[]{:S(2)}) async-start(), calls=%async_computation.55 | async-start | bytes 7864320 | tf_op jit(solution)/shard_map/all_gather | solution.py:208
  111.5 396.1 %all-gather.31.cloned.1.call-start = ((), (), s32[]{:S(2)}) async-start(), calls=%async_computation.56 | async-start | bytes 7864320 | tf_op jit(solution)/shard_map/all_gather | solution.py:209
  229.6 393.0 %all-gather.33.cloned.1.call-start = ((), (), s32[]{:S(2)}) async-start(), calls=%async_computation.57 | async-start | bytes 2359296 | tf_op jit(solution)/shard_map/all_gather | solution.py:251
  255.0 370.2 %all-gather.35.cloned.1.call-start = ((), (), s32[]{:S(2)}) async-start(), calls=%async_computation.58 | async-start | bytes 2359296 | tf_op jit(solution)/shard_map/all_gather | solution.py:250
  974.8 288.5 %reduce-scatter.39.cloned.1.call-start = ((), (), s32[]{:S(2)}) async-start(), calls=%async_computation.60 | async-start | bytes 2359296 | tf_op jit(solution)/shard_map/reduce_scatter | solution.py:580
  1033.6 235.1 %reduce-scatter.37.cloned.1.call-start = ((), (), s32[]{:S(2)}) async-start(), calls=%async_computation.59 | async-start | bytes 2359296 | tf_op jit(solution)/shard_map/reduce_scatter | solution.py:574
  1042.3 292.7 %reduce-scatter.43.cloned.1.call-start = ((), (), s32[]{:S(2)}) async-start(), calls=%async_computation.62 | async-start | bytes 2359296 | tf_op jit(solution)/shard_map/reduce_scatter | solution.py:580
  1135.9 223.9 %reduce-scatter.41.cloned.1.call-start = ((), (), s32[]{:S(2)}) async-start(), calls=%async_computation.61 | async-start | bytes 2359296 | tf_op jit(solution)/shard_map/reduce_scatter | solution.py:574
  1181.2 275.5 %reduce-scatter.57.cloned.1.call-start = ((), (), s32[]{:S(2)}) async-start(), calls=%async_computation.69 | async-start | bytes 1474560 | tf_op jit(solution)/shard_map/reduce_scatter | solution.py:674
  1233.3 223.5 %reduce-scatter.59.cloned.1.call-start = ((), (), s32[]{:S(2)}) async-start(), calls=%async_computation.70 | async-start | bytes 1474560 | tf_op jit(solution)/shard_map/reduce_scatter | solution.py:674
  1239.6 219.0 %reduce-scatter.53.cloned.1.call-start = ((), (), s32[]{:S(2)}) async-start(), calls=%async_computation.67 | async-start | bytes 1474560 | tf_op jit(solution)/shard_map/reduce_scatter | solution.py:671
  1329.8 128.8 %reduce-scatter.55.cloned.1.call-start = ((), (), s32[]{:S(2)}) async-start(), calls=%async_computation.68 | async-start | bytes 1474560 | tf_op jit(solution)/shard_map/reduce_scatter | solution.py:671
  1340.4 120.1 %reduce-scatter.45.cloned.1.call-start = ((), (), s32[]{:S(2)}) async-start(), calls=%async_computation.63 | async-start | bytes 1474560 | tf_op jit(solution)/shard_map/reduce_scatter | solution.py:665
  1380.5 109.5 %reduce-scatter.51.cloned.1.call-start = ((), (), s32[]{:S(2)}) async-start(), calls=%async_computation.66 | async-start | bytes 1474560 | tf_op jit(solution)/shard_map/reduce_scatter | solution.py:668
  1384.4 217.1 %reduce-scatter.65.cloned.1.call-start = ((), (), s32[]{:S(2)}) async-start(), calls=%async_computation.73 | async-start | bytes 7864320 | tf_op jit(solution)/shard_map/reduce_scatter | solution.py:692
  1394.7 320.5 %reduce-scatter.67.cloned.1.call-start = ((), (), s32[]{:S(2)}) async-start(), calls=%async_computation.74 | async-start | bytes 7864320 | tf_op jit(solution)/shard_map/reduce_scatter | solution.py:692
  1404.5 424.1 %reduce-scatter.69.cloned.1.call-start = ((), (), s32[]{:S(2)}) async-start(), calls=%async_computation.75 | async-start | bytes 7864320 | tf_op jit(solution)/shard_map/reduce_scatter | solution.py:695
  1414.1 527.9 %reduce-scatter.71.cloned.1.call-start = ((), (), s32[]{:S(2)}) async-start(), calls=%async_computation.76 | async-start | bytes 7864320 | tf_op jit(solution)/shard_map/reduce_scatter | solution.py:695
  1423.6 632.1 %reduce-scatter.61.cloned.1.call-start = ((), (), s32[]{:S(2)}) async-start(), calls=%async_computation.71 | async-start | bytes 7864320 | tf_op jit(solution)/shard_map/reduce_scatter | solution.py:689
  1433.7 735.6 %reduce-scatter.63.cloned.1.call-start = ((), (), s32[]{:S(2)}) async-start(), calls=%async_computation.72 | async-start | bytes 7864320 | tf_op jit(solution)/shard_map/reduce_scatter | solution.py:689
  1443.7 747.8 %reduce-scatter.81.cloned.1.call-start = ((), (), s32[]{:S(2)}) async-start(), calls=%async_computation.81 | async-start | bytes 245760
  1445.2 766.5 %reduce-scatter.77.cloned.1.call-start = ((), (), s32[]{:S(2)}) async-start(), calls=%async_computation.79 | async-start | bytes 245760
  1448.5 783.3 %reduce-scatter.73.cloned.1.call-start = ((), (), s32[]{:S(2)}) async-start(), calls=%async_computation.77 | async-start | bytes 245760
  1450.1 801.6 %reduce-scatter.83.cloned.1.call-start = ((), (), s32[]{:S(2)}) async-start(), calls=%async_computation.82 | async-start | bytes 245760
  1451.7 820.1 %reduce-scatter.79.cloned.1.call-start = ((), (), s32[]{:S(2)}) async-start(), calls=%async_computation.80 | async-start | bytes 245760
  1455.0 836.9 %reduce-scatter.75.cloned.1.call-start = ((), (), s32[]{:S(2)}) async-start(), calls=%async_computation.78 | async-start | bytes 245760
  1456.7 894.8 %all-reduce.14.cloned.1.call-start = ((), (), s32[]{:S(2)}) async-start(), calls=%async_computation.83 | async-start | bytes 2359296 | tf_op jit(solution)/shard_map/psum | solution.py:716
  1491.8 890.7 %all-reduce.16.cloned.1.call-start = ((), (), s32[]{:S(2)}) async-start(), calls=%async_computation.84 | async-start | bytes 9437184 | tf_op jit(solution)/shard_map/psum | solution.py:726
  (304 other events, 4396.9 us)
Sparse Core Ops, SparseCore 0:
  9.6 33.1 all-gather.20
  44.3 29.4 all-gather.18
  75.3 29.4 all-gather.14
  106.3 9.0 all-gather.22
  116.7 10.9 all-gather.16
  129.1 32.0 all-gather.24
  162.8 114.4 all-gather.26
  278.9 113.5 all-gather.28
  394.0 113.5 all-gather.30
  518.5 10.9 all-gather.34
  1186.1 27.8 reduce-scatter.56
  1239.7 27.8 reduce-scatter.58
  1269.8 27.9 reduce-scatter.52
  1340.5 27.8 reduce-scatter.54
  1372.8 25.6 reduce-scatter.44
  1401.4 27.9 reduce-scatter.46
  1431.7 27.9 reduce-scatter.48
  1462.0 27.9 reduce-scatter.50
  1492.1 109.3 reduce-scatter.64
  1603.8 111.2 reduce-scatter.66
  1717.3 111.2 reduce-scatter.68
  1830.7 111.2 reduce-scatter.70
  1944.3 111.2 reduce-scatter.60
  2058.0 111.2 reduce-scatter.62
  2171.4 20.0 reduce-scatter.80
  2193.8 17.8 reduce-scatter.76
  2213.9 17.8 reduce-scatter.72
  2233.9 17.7 reduce-scatter.82
  2254.0 17.7 reduce-scatter.78
  2274.1 17.8 reduce-scatter.74
  2295.8 55.6 all-reduce.13
  2354.1 28.3 all-reduce.15
  (5 shorter events, 35.2 us)
where the time goes:
time: 2410 us; the launch traced here: 2400 us
  waiting for transfers between devices  1090 us (45%)
  matrix products  468 us (19%)
  local copies, waits for them, and re-layouts  321 us (13%)
  other arithmetic  308 us (13%)
  starting transfers between devices  97.7 us (4%)
  blocking collectives  87.9 us (4%)
    reduce_scatter x2, waiting for transfers between devices, per_device(): lax.psum_scatter(complete[9].astype(jnp.bfloat16), 'dp', scatter_dimensio...  224 us
    reduce_scatter x2, waiting for transfers between devices, per_device(): lax.psum_scatter(complete[11].astype(jnp.bfloat16), 'dp', scatter_dimensi...  223 us
    reduce_scatter x2, waiting for transfers between devices, per_device(): lax.psum_scatter(complete[10].astype(jnp.bfloat16), 'dp', scatter_dimensi...  223 us
    unnamed x43, waiting for transfers between devices  114 us
    all_gather x1, waiting for transfers between devices, per_device(): lax.all_gather(expert_down, 'dp', axis=1, tiled=True)  80.9 us
    unnamed x581, local copies, waits for them, and re-layouts  49.1 us
    dot_general x4, matrix products, attend_backward(): jnp.einsum('bqhd,bkhd->bhqk', grad_out, value_rows, preferred_element_typ...  49 us
  transfers between devices with their start and end apart: 60, of which 34 were waited for; matrix products, arithmetic and copies ran while one was open for 35% of the time, Pallas kernels for 0%

commit v1 on v0

v1 whole, which is shorter than its diff:
```python
import jax
import jax.numpy as jnp
from jax import lax
from jax.experimental import pallas as pl
from jax.experimental.pallas import tpu as pltpu
from jax.sharding import PartitionSpec as P

HEADS = 12
HEAD_DIM = 64
PROMPT = 1024
CONT_LEN = 128

precise = lax.Precision.HIGHEST
epsilon = 1e-06
negative = -1e30
scale_factor = 0.125
f32 = jnp.float32
bf16 = jnp.bfloat16


def dot(a, b):
    return jnp.dot(a, b, preferred_element_type=f32)


def dot_nt(a, b):
    return lax.dot_general(a, b, (((a.ndim - 1,), (b.ndim - 1,)), ((), ())), preferred_element_type=f32)


def dot_tn(a, b):
    return lax.dot_general(a, b, (((0,), (0,)), ((), ())), preferred_element_type=f32)


QB = 256
LANES = 128


def turn(t, cos, sin, sign):
    lane = lax.broadcasted_iota(jnp.int32, t.shape, 1)
    partner = jnp.where(lane % HEAD_DIM < HEAD_DIM // 2, pltpu.roll(t, 96, 1), pltpu.roll(t, 32, 1))
    return t * cos + sign * (partner * sin)


def qkv_kernel(x_ref, gain_ref, w_ref, cos_ref, sin_ref, qkv_ref, in_ref):
    x = x_ref[0].astype(f32)
    inv = lax.rsqrt(jnp.mean(x * x, axis=-1, keepdims=True) + epsilon)
    a = (x * inv * gain_ref[...]).astype(bf16)
    in_ref[0] = a
    cos = cos_ref[...]
    sin = sin_ref[...]
    for c in range(w_ref.shape[1] // LANES):
        cols = slice(c * LANES, (c + 1) * LANES)
        t = dot(a, w_ref[:, cols])
        if c % 3 < 2:
            t = turn(t, cos, sin, 1.0)
        qkv_ref[0, :, cols] = t.astype(bf16)


def qkv_call(x, gain, w, cos, sin):
    m, rows, d = x.shape
    width = w.shape[1] // (3 * LANES) * 3 * LANES
    half = rows // 2
    return pl.pallas_call(
        qkv_kernel,
        grid=(m, 2),
        in_specs=[
            pl.BlockSpec((1, half, d), lambda i, j: (i, j, 0)),
            pl.BlockSpec((1, d), lambda i, j: (0, 0)),
            pl.BlockSpec((d, width), lambda i, j: (0, 0)),
            pl.BlockSpec((half, LANES), lambda i, j: (j, 0)),
            pl.BlockSpec((half, LANES), lambda i, j: (j, 0)),
        ],
        out_specs=[
            pl.BlockSpec((1, half, width), lambda i, j: (i, j, 0)),
            pl.BlockSpec((1, half, d), lambda i, j: (i, j, 0)),
        ],
        out_shape=[jax.ShapeDtypeStruct((m, rows, width), bf16), jax.ShapeDtypeStruct((m, rows, d), bf16)],
        name="qkv",
    )(x, gain, w, cos, sin)


def head_mask(t, h):
    lane = lax.broadcasted_iota(jnp.int32, t.shape, 1)
    return jnp.where(lane // HEAD_DIM == h, t, jnp.zeros_like(t))


def last_block_mask(i, blocks):
    r = lax.broadcasted_iota(jnp.int32, (QB, QB), 0)
    c = lax.broadcasted_iota(jnp.int32, (QB, QB), 1)
    see = r <= c
    if i == blocks:
        see = see & (r // CONT_LEN == c // CONT_LEN)
    return see


def flip(t):
    return t.astype(f32).T.astype(bf16)


def attend_kernel(qkv_ref, o_ref, lse_ref):
    rows = qkv_ref.shape[1]
    blocks = PROMPT // QB
    k = qkv_ref[0, :, LANES : 2 * LANES]
    vt = flip(qkv_ref[0, :, 2 * LANES :])
    for i in range(rows // QB):
        n = (i + 1) * QB
        q = qkv_ref[0, i * QB : n, :LANES].astype(f32) * scale_factor
        see = last_block_mask(i, blocks)
        outs = []
        for h in range(2):
            qm = head_mask(q, h).astype(bf16)
            s_last = jnp.where(see, dot_nt(k[n - QB : n], qm), negative)
            s = s_last if i == 0 else jnp.concatenate([dot_nt(k[: n - QB], qm), s_last], axis=0)
            top = jnp.max(s, axis=0, keepdims=True)
            p = jnp.exp(s - top)
            total = jnp.sum(p, axis=0, keepdims=True)
            ot = dot(vt[h * HEAD_DIM : (h + 1) * HEAD_DIM, :n], p.astype(bf16))
            outs.append(ot / total)
            lse_ref[0, 0, h : h + 1, i * QB : n] = top + jnp.log(total)
        o_ref[0, i * QB : n, :] = jnp.concatenate(outs, axis=0).T.astype(bf16)


def attend_call(qkv):
    m, rows, width = qkv.shape
    pairs = width // (3 * LANES)
    return pl.pallas_call(
        attend_kernel,
        grid=(m, pairs),
        in_specs=[pl.BlockSpec((1, rows, 3 * LANES), lambda i, j: (i, 0, j))],
        out_specs=[
            pl.BlockSpec((1, rows, LANES), lambda i, j: (i, 0, j)),
            pl.BlockSpec((1, 1, 2, rows), lambda i, j: (i, j, 0, 0)),
        ],
        out_shape=[
            jax.ShapeDtypeStruct((m, rows, pairs * LANES), bf16),
            jax.ShapeDtypeStruct((m, pairs, 2, rows), f32),
        ],
        name="attend",
    )(qkv)


def attend_back_kernel(qkv_ref, do_p_ref, do_v_ref, lse_ref, cos_ref, sin_ref, low_ref, dk_ref, dv_ref):
    rows = qkv_ref.shape[1]
    blocks = PROMPT // QB
    k = qkv_ref[0, :, LANES : 2 * LANES]
    v = qkv_ref[0, :, 2 * LANES :]
    kt = flip(k)
    dk_ref[...] = jnp.zeros_like(dk_ref)
    dv_ref[...] = jnp.zeros_like(dv_ref)
    for i in range(rows // QB):
        n = (i + 1) * QB
        own = slice(i * QB, n)
        q = qkv_ref[0, own, :LANES].astype(f32) * scale_factor
        do = (do_p_ref[0, own, :] if i < blocks else do_v_ref[0, (i - blocks) * QB : (i - blocks + 1) * QB, :]).astype(f32)
        see = last_block_mask(i, blocks)
        outs = []
        for h in range(2):
            qm = head_mask(q, h).astype(bf16)
            dom = head_mask(do, h).astype(bf16)
            s_last = jnp.where(see, dot_nt(k[n - QB : n], qm), negative)
            s = s_last if i == 0 else jnp.concatenate([dot_nt(k[: n - QB], qm), s_last], axis=0)
            p = jnp.exp(s - lse_ref[0, 0, h : h + 1, own])
            dp = dot_nt(v[:n], dom)
            ds = (p * (dp - jnp.sum(dp * p, axis=0, keepdims=True))).astype(bf16)
            dv_ref[:n, :] += dot(p.astype(bf16), dom)
            dk_ref[:n, :] += dot(ds, qm)
            outs.append(dot(kt[h * HEAD_DIM : (h + 1) * HEAD_DIM, :n], ds))
        dq = jnp.concatenate(outs, axis=0).T * scale_factor
        low_ref[0, own, :LANES] = turn(dq, cos_ref[own, :], sin_ref[own, :], -1.0).astype(bf16)
    low_ref[0, :, LANES : 2 * LANES] = turn(dk_ref[...], cos_ref[...], sin_ref[...], -1.0).astype(bf16)
    low_ref[0, :, 2 * LANES :] = dv_ref[...].astype(bf16)


def attend_back_call(qkv, do_p, do_v, lse, cos, sin):
    m, rows, width = qkv.shape
    pairs = width // (3 * LANES)
    return pl.pallas_call(
        attend_back_kernel,
        grid=(m, pairs),
        in_specs=[
            pl.BlockSpec((1, rows, 3 * LANES), lambda i, j: (i, 0, j)),
            pl.BlockSpec((1, do_p.shape[1], LANES), lambda i, j: (i, 0, j)),
            pl.BlockSpec((1, do_v.shape[1], LANES), lambda i, j: (i, 0, j)),
            pl.BlockSpec((1, 1, 2, rows), lambda i, j: (i, j, 0, 0)),
            pl.BlockSpec((rows, LANES), lambda i, j: (0, 0)),
            pl.BlockSpec((rows, LANES), lambda i, j: (0, 0)),
        ],
        out_specs=pl.BlockSpec((1, rows, 3 * LANES), lambda i, j: (i, 0, j)),
        out_shape=jax.ShapeDtypeStruct((m, rows, width), bf16),
        scratch_shapes=[pltpu.VMEM((rows, LANES), f32), pltpu.VMEM((rows, LANES), f32)],
        name="attend_back",
    )(qkv, do_p, do_v, lse, cos, sin)


def din_kernel(low_ref, w_ref, x_ref, d_ref, gain_ref):
    @pl.when((pl.program_id(0) == 0) & (pl.program_id(1) == 0))
    def _():
        gain_ref[...] = jnp.zeros_like(gain_ref)

    d = dot_nt(low_ref[0], w_ref[...])
    x = x_ref[0].astype(f32)
    inv = lax.rsqrt(jnp.mean(x * x, axis=-1, keepdims=True) + epsilon)
    gain_ref[...] += jnp.sum(d * (x * inv), axis=0, keepdims=True)
    d_ref[0] = d.astype(bf16)


def din_call(low, w, x):
    m, rows, width = low.shape
    d = x.shape[2]
    half = rows // 2
    return pl.pallas_call(
        din_kernel,
        grid=(m, 2),
        in_specs=[
            pl.BlockSpec((1, half, width), lambda i, j: (i, j, 0)),
            pl.BlockSpec((d, width), lambda i, j: (0, 0)),
            pl.BlockSpec((1, half, d), lambda i, j: (i, j, 0)),
        ],
        out_specs=[
            pl.BlockSpec((1, half, d), lambda i, j: (i, j, 0)),
            pl.BlockSpec((1, d), lambda i, j: (0, 0)),
        ],
        out_shape=[jax.ShapeDtypeStruct((m, rows, d), bf16), jax.ShapeDtypeStruct((1, d), f32)],
        name="din",
    )(low, w, x)


def per_device(
    tokens,
    previous_gate,
    routes,
    prompt_choice,
    attention_gain,
    query_weight,
    key_weight,
    value_weight,
    output_weight,
    feedforward_gain,
    router_weight,
    constant_weight,
    constant_vector,
    expert_gate,
    expert_up,
    expert_down,
    cotangent,
):
    MB, R, D = tokens.shape[0], tokens.shape[3], tokens.shape[4]
    C = prompt_choice.shape[3]
    E = lax.axis_size("expert")
    S = lax.axis_size("seq")
    PH = PROMPT // S
    CR = C * CONT_LEN
    cap = R // 4
    local_experts = expert_gate.shape[0]
    all_experts = local_experts * E
    routes_n = all_experts + 4
    HW = D // S
    e_index = lax.axis_index("expert")
    s_index = lax.axis_index("seq")
    shard = query_weight.shape[0]
    dense_axes = ("dp", "expert")
    all_axes = ("dp", "expert", "seq")
    pair = ("expert", "seq")

    toks = tokens[:, 0, 0]
    cont_toks = lax.all_gather(toks[:, PH:].reshape(MB, C, CONT_LEN, D), pair, axis=0)
    prompt_toks = lax.all_gather(toks[:, :PH], "seq", axis=1, tiled=True)
    choices = lax.all_gather(prompt_choice[:, 0, 0], pair, axis=0)
    choices = choices.transpose(1, 0, 2).reshape(MB, E * S * C)
    chosen_i = (choices[:, :, None] == jnp.arange(E)[None, None, :]).astype(jnp.int32)
    rank = jnp.sum((jnp.cumsum(chosen_i, axis=1) - chosen_i) * chosen_i, axis=2)
    slots = S * C
    n_cont = E * S * C
    here = choices == e_index
    at_slot = here[:, None, :] & (rank[:, None, :] == jnp.arange(slots)[None, :, None])
    visit_id = jnp.sum(jnp.where(at_slot, jnp.arange(n_cont), 0), axis=2)
    visit_row = ((visit_id // C) * MB + jnp.arange(MB)[:, None]) * C + visit_id % C
    my_choice = prompt_choice[:, 0, 0]

    def pick_visitors(t):
        w = t.shape[-1]
        return jnp.take(t.reshape(E * S * MB * C, CONT_LEN, w), visit_row.reshape(-1), axis=0).reshape(MB, slots * CONT_LEN, w)

    def send_home(t):
        w = t.shape[-1]
        t = t.reshape(MB, slots, 1, CONT_LEN, w)
        marks = at_slot.reshape(MB, slots, n_cont, 1, 1)
        zero = jnp.zeros((), t.dtype)
        out = jnp.where(marks[:, 0], t[:, 0], zero)
        for j in range(1, slots):
            out = jnp.where(marks[:, j], t[:, j], out)
        out = out.reshape(MB, E * S, C, CONT_LEN, w).transpose(1, 0, 2, 3, 4)
        return lax.all_to_all(out, pair, split_axis=0, concat_axis=0, tiled=True)

    rows_all = jnp.concatenate([prompt_toks, pick_visitors(cont_toks)], axis=1)

    n16 = shard // E
    half_shard = shard // S

    def mine(w):
        return lax.dynamic_slice(w, (0, s_index * HW), (shard, HW)).reshape(shard, HW // LANES, 1, LANES)

    part_a = jnp.concatenate(
        [
            jnp.concatenate([mine(query_weight), mine(key_weight), mine(value_weight)], axis=2).reshape(shard, 3 * HW),
            jnp.pad(attention_gain[:, None], ((0, 0), (0, LANES - 1))),
        ],
        axis=1,
    )
    n_dp = lax.axis_size("dp")
    full_a = lax.all_to_all(
        jnp.broadcast_to(part_a[None], (n_dp,) + part_a.shape), "dp", split_axis=0, concat_axis=0, tiled=True
    ).reshape(D, 3 * HW + LANES)
    gain_attn = full_a[:, 3 * HW].astype(f32)
    small_cols = routes_n + 4 + 1 + 2
    part_b = jnp.concatenate(
        [
            output_weight,
            router_weight,
            constant_weight,
            feedforward_gain[:, None],
            constant_vector.T,
            jnp.zeros((shard, LANES - small_cols), bf16),
        ],
        axis=1,
    )
    part_b = lax.dynamic_slice(part_b, (s_index * half_shard, 0), (half_shard, D + LANES))
    full_b = lax.all_gather(part_b, ("dp", "seq"), axis=0, tiled=True)
    w_out = full_b[:, :D]
    w_small = full_b[:, D : D + routes_n + 4]
    gain_ffn = full_b[:, D + routes_n + 4].astype(f32)
    vectors = full_b[:, D + routes_n + 5 : D + routes_n + 7].astype(f32).T

    def own_expert(w):
        return lax.dynamic_index_in_dim(w, s_index, 0, keepdims=False)

    w_gate = lax.all_gather(own_expert(expert_gate), "dp", axis=0, tiled=True)
    w_up = lax.all_gather(own_expert(expert_up), "dp", axis=0, tiled=True)
    w_down = lax.all_gather(own_expert(expert_down), "dp", axis=0, tiled=True)

    inverse = 10000.0 ** (-jnp.arange(HEAD_DIM // 2, dtype=f32) * 2.0 / HEAD_DIM)
    pos = jnp.concatenate([jnp.arange(PROMPT), PROMPT + jnp.arange(slots * CONT_LEN) % CONT_LEN])
    angle = pos.astype(f32)[:, None] * inverse
    cos = jnp.concatenate([jnp.cos(angle)] * 4, axis=-1)
    sin = jnp.concatenate([-jnp.sin(angle), jnp.sin(angle)] * 2, axis=-1)
    qkv, attn_in = qkv_call(rows_all, gain_attn[None], full_a, cos, sin)
    heads_out, lse = attend_call(qkv)
    prompt_out = heads_out[:, :PROMPT].reshape(MB, S, PH, HW).transpose(1, 0, 2, 3)
    prompt_out = lax.all_to_all(prompt_out, "seq", split_axis=0, concat_axis=0, tiled=True)
    cont_out = jnp.sum(send_home(heads_out[:, PROMPT:]).reshape(E, S, MB, CR, HW), axis=0)
    attn = jnp.concatenate([prompt_out, cont_out], axis=2)
    attn_low = jnp.concatenate([attn[i] for i in range(S)], axis=-1).reshape(MB * R, D)
    N = MB * R
    x = toks.reshape(N, D).astype(f32)
    h = x + dot(attn_low, w_out)
    inv2 = lax.rsqrt(jnp.mean(h * h, axis=-1, keepdims=True) + epsilon)
    hhat = h * inv2
    normed = hhat * gain_ffn
    normed_low = normed.astype(bf16)
    dy_low = cotangent[:, 0, 0].reshape(N, D)
    dy = dy_low.astype(f32)

    route = routes[:, 0, 0].reshape(N, 2)
    marks = (route[:, :, None] == jnp.arange(routes_n)).astype(f32)
    small = dot(normed_low, w_small)
    logits = small[:, :routes_n] + previous_gate[:, 0, 0].reshape(N, routes_n)
    chosen_logits = jnp.sum(logits[:, None, :] * marks, axis=-1)
    gate = jax.nn.softmax(chosen_logits, axis=-1)
    alphas = jax.nn.softmax(small[:, routes_n:].reshape(N, 2, 2), axis=-1)
    lower = (jnp.arange(R)[None, :] < jnp.arange(R)[:, None]).astype(bf16)
    marks_low = marks.astype(bf16).reshape(MB, R, 2 * routes_n)
    before = jnp.einsum("rs,msk->mrk", lower, marks_low, preferred_element_type=f32).reshape(MB, R, 2, routes_n)
    first_count = jnp.sum(marks.reshape(MB, R, 2, routes_n)[:, :, 0], axis=1)
    before = before + jnp.stack([jnp.zeros_like(first_count), first_count], axis=1)[:, None]
    ranks = jnp.sum(before.reshape(N, 2, routes_n) * marks, axis=-1).astype(jnp.int32)
    is_ffn = route < all_experts
    index = jnp.where(is_ffn, route * cap + ranks, -1).reshape(MB, R, 2)
    n_slots = all_experts * cap
    onehot = [(index[:, :, i, None] == jnp.arange(n_slots)).astype(bf16) for i in range(2)]
    both = onehot[0] + onehot[1]
    sent_rows = jnp.einsum("mrs,mrd->msd", both, normed_low.reshape(MB, R, D), preferred_element_type=f32).astype(bf16)
    sent_dy = jnp.einsum("mrs,mrd->msd", both, dy_low.reshape(MB, R, D), preferred_element_type=f32)
    gate_m = gate.reshape(MB, R, 2)
    slot_gate = jnp.sum(
        jnp.where(onehot[0] > 0, gate_m[:, :, 0:1], 0.0) + jnp.where(onehot[1] > 0, gate_m[:, :, 1:2], 0.0), axis=1
    )
    sent_dy = (sent_dy * slot_gate[:, :, None]).astype(bf16)

    def to_experts(t):
        return lax.all_to_all(t.reshape(all_experts, cap, D), pair, split_axis=0, concat_axis=0, tiled=True)

    results = []
    back = []
    sums = None
    for m in range(MB):
        rows = to_experts(sent_rows[m]).reshape(-1, D)
        grads = to_experts(sent_dy[m]).reshape(-1, D)
        gate_pre = dot(rows, w_gate)
        up_pre = dot(rows, w_up)
        sig = jax.nn.sigmoid(gate_pre)
        act = gate_pre * sig
        hidden = (act * up_pre).astype(bf16)
        out = dot(hidden, w_down).astype(bf16)
        dhid = dot_nt(grads, w_down)
        d_up = (dhid * act).astype(bf16)
        d_gate = (dhid * up_pre * sig * (1.0 + gate_pre * (1.0 - sig))).astype(bf16)
        d_rows = (dot_nt(d_gate, w_gate) + dot_nt(d_up, w_up)).astype(bf16)
        parts = (dot_tn(rows, d_gate), dot_tn(rows, d_up), dot_tn(hidden, grads))
        sums = parts if sums is None else tuple(a + b for a, b in zip(sums, parts))
        results.append(to_experts(out).reshape(n_slots, D))
        back.append(to_experts(d_rows).reshape(n_slots, D))

    def scatter_dp(g):
        return lax.psum_scatter(g.astype(bf16), "dp", scatter_dimension=0, tiled=True)

    expert_parts = [scatter_dp(g) for g in sums]
    expert_outs = [lax.all_gather(g, "seq", axis=0).astype(f32) for g in expert_parts]

    ffn = [
        jnp.stack([dot(onehot[i][m], results[m]) for m in range(MB)]).reshape(N, D) for i in range(2)
    ]
    d_ffn = jnp.stack([dot(both[m], back[m]) for m in range(MB)]).reshape(N, D)
    const = [alphas[:, c, 0:1] * normed + alphas[:, c, 1:2] * vectors[c] for c in range(2)]
    mark_of = lambda i, r: marks[:, i, r : r + 1]
    branch = [
        ffn[i]
        + mark_of(i, all_experts + 1) * normed
        + mark_of(i, all_experts + 2) * const[0]
        + mark_of(i, all_experts + 3) * const[1]
        for i in range(2)
    ]
    mixed = h + gate[:, 0:1] * branch[0] + gate[:, 1:2] * branch[1]
    d_gates = jnp.stack([jnp.sum(dy * b, axis=-1) for b in branch], axis=-1)
    d_chosen = gate * (d_gates - jnp.sum(gate * d_gates, axis=-1, keepdims=True))
    d_logits = jnp.sum(d_chosen[:, :, None] * marks, axis=1)
    weight_of = lambda r: jnp.sum(gate * marks[:, :, r], axis=-1, keepdims=True)
    dn = d_ffn + weight_of(all_experts + 1) * dy
    dz = []
    d_vec = []
    dyn = jnp.sum(dy * normed, axis=-1, keepdims=True)
    for c in range(2):
        wt = weight_of(all_experts + 2 + c)
        dn = dn + alphas[:, c, 0:1] * wt * dy
        d_alpha = jnp.concatenate([wt * dyn, wt * jnp.sum(dy * vectors[c], axis=-1, keepdims=True)], axis=-1)
        dz.append(alphas[:, c] * (d_alpha - jnp.sum(alphas[:, c] * d_alpha, axis=-1, keepdims=True)))
        d_vec.append(jnp.sum(alphas[:, c, 1:2] * wt * dy, axis=0))
    d_small = jnp.concatenate([d_logits] + dz, axis=1)
    g_small = jnp.dot(normed_low.astype(f32).T, d_small, precision=precise)
    dn = dn + jnp.dot(d_small, w_small.astype(f32).T, precision=precise)
    g_gain_ffn = jnp.sum(dn * hhat, axis=0)
    u = dn * gain_ffn
    dh = dy + inv2 * (u - hhat * jnp.mean(u * hhat, axis=-1, keepdims=True))
    dh_low = dh.astype(bf16)
    g_out = dot_tn(attn_low, dh_low)
    cols = jnp.concatenate(
        [g_out, g_small, g_gain_ffn[:, None], d_vec[0][:, None], d_vec[1][:, None], jnp.zeros((D, LANES - routes_n - 7), f32)],
        axis=1,
    ).astype(bf16)

    def sum_shards(t, axes, count):
        t = lax.all_to_all(t.reshape(count, t.shape[0] // count, t.shape[1]), axes, split_axis=0, concat_axis=0, tiled=True)
        return jnp.sum(t.astype(f32), axis=0).astype(bf16)

    red_b = sum_shards(cols, all_axes, n_dp * E * S)
    red_b = lax.all_gather(red_b, pair, axis=0, tiled=True).astype(f32)
    d_attn = jnp.stack([dot_nt(dh_low, w_out[i * HW : (i + 1) * HW]) for i in range(S)]).astype(bf16)
    d_attn = d_attn.reshape(S, MB, R, HW)
    d_cont = d_attn[:, :, PH:].reshape(1, S, MB, C, CONT_LEN, HW)
    goes = my_choice[None] == jnp.arange(E)[:, None, None]
    d_cont = jnp.where(goes[:, None, :, :, None, None], d_cont, jnp.zeros((), bf16)).reshape(E * S, MB, C, CONT_LEN, HW)
    d_vis = pick_visitors(lax.all_to_all(d_cont, pair, split_axis=0, concat_axis=0, tiled=True))
    d_prompt = lax.all_to_all(d_attn[:, :, :PH], "seq", split_axis=0, concat_axis=0, tiled=True)
    d_prompt = d_prompt.transpose(1, 0, 2, 3).reshape(MB, PROMPT, HW)
    low = attend_back_call(qkv, d_prompt, d_vis, lse, cos, sin)
    d_in, gain_part = din_call(low, full_a, rows_all)
    g_qkv = dot_tn(attn_in.reshape(-1, D), low.reshape(-1, 3 * HW))
    red_a = jnp.concatenate([g_qkv, jnp.pad(gain_part.T, ((0, 0), (0, LANES - 1)))], axis=1).astype(bf16)
    red_a = sum_shards(red_a, dense_axes, n_dp * E)
    red_a = lax.all_gather(red_a, pair, axis=0).astype(f32)
    g_gain_attn = jnp.sum(red_a[:, :, 3 * HW].reshape(E, S, n16), axis=1).reshape(shard)
    red_a = red_a[:, :, : 3 * HW].reshape(E, S, n16, HW // LANES, 3, LANES)
    red_a = red_a.transpose(4, 0, 2, 1, 3, 5).reshape(3, shard, D)
    d_cont = jnp.sum(send_home(d_in[:, PROMPT:]).astype(f32), axis=0).reshape(MB, CR, D)
    d_halves = d_in[:, :PROMPT].reshape(MB, S, PH, D)
    own = lax.dynamic_index_in_dim(d_halves, s_index, 1, keepdims=False)
    other = lax.dynamic_index_in_dim(d_halves, 1 - s_index, 1, keepdims=False)
    swap = [(i, (i + 1) % S) for i in range(S)]
    d_own = own.astype(f32) + lax.ppermute(other, "seq", swap).astype(f32)
    d_in = jnp.concatenate([d_own, d_cont], axis=1).reshape(N, D)
    inv1 = lax.rsqrt(jnp.mean(x * x, axis=-1, keepdims=True) + epsilon)
    xhat = x * inv1
    u1 = d_in * gain_attn
    d_input = dh + inv1 * (u1 - xhat * jnp.mean(u1 * xhat, axis=-1, keepdims=True))

    o = D + routes_n
    return (
        mixed.astype(bf16).reshape(MB, 1, 1, R, D),
        d_input.reshape(MB, 1, 1, R, D),
        g_gain_attn,
        red_a[0],
        red_a[1],
        red_a[2],
        red_b[:, :D],
        red_b[:, o + 4],
        red_b[:, D:o],
        red_b[:, o : o + 4],
        red_b[:, o + 5 : o + 7].T,
        expert_outs[0],
        expert_outs[1],
        expert_outs[2],
    )


def solution(mesh):
    rows = P(None, ("dp", "expert"), "seq", None, None)
    in_specs = (
        rows,
        rows,
        rows,
        P(None, ("dp", "expert"), "seq", None),
        P("dp"),
        P("dp", None),
        P("dp", None),
        P("dp", None),
        P("dp", None),
        P("dp"),
        P("dp", None),
        P("dp", None),
        P(None, "dp"),
        P("expert", "dp", None),
        P("expert", "dp", None),
        P("expert", "dp", None),
        rows,
    )
    out_specs = (
        rows,
        rows,
        P("dp"),
        P("dp", None),
        P("dp", None),
        P("dp", None),
        P("dp", None),
        P("dp"),
        P("dp", None),
        P("dp", None),
        P(None, "dp"),
        P("expert", "dp", None),
        P("expert", "dp", None),
        P("expert", "dp", None),
    )
    return jax.shard_map(per_device, mesh=mesh, in_specs=in_specs, out_specs=out_specs, check_vma=False)
```

time: 2410 us -> 765 us (0.32)
  waiting for transfers between devices: 1090 us -> 145 us
  matrix products: 468 us -> 221 us
  local copies, waits for them, and re-layouts: 321 us -> 76.8 us
  other arithmetic: 308 us -> 86.7 us
  Pallas kernels: 0 us -> 100 us
  blocking collectives: 87.9 us -> 36.5 us
  starting transfers between devices: 97.7 us -> 72.1 us
    reduce_scatter x18 -> x3, waiting for transfers between devices: 698 us -> 0.03 us  [scatter_dp(): lax.psum_scatter(g.astype(bf16), 'dp', scatter_dimension=0, tiled=True)]
    dot_general x92 -> x35, matrix products: 468 us -> 221 us  [the longest x14 80.6 us: dot(): return jnp.dot(a, b, preferred_element_type=f32)]
    convert_element_type x55 -> x12, other arithmetic: 140 us -> 13.5 us  [the longest x3 10.3 us: per_device(): lax.all_gather(g, 'seq', axis=0).astype(f32)]
    all_gather x11 -> x9, waiting for transfers between devices: 142 us -> 18.4 us  [the longest x1 18.4 us: per_device(): w_down = lax.all_gather(own_expert(expert_down), 'dp', axis=0, tiled=True)]
    unnamed x43 -> x12, waiting for transfers between devices: 114 us -> 0.2 us
    mul x34 -> x0, local copies, waits for them, and re-layouts: 107 us -> none  [the longest x12 33.6 us: per_device(): const_mask[:, :, 0:1] * const_out[:, None, 0]]
    pallas_call x0 -> x4, Pallas kernels: none -> 100 us  [the longest x1 46.6 us: attend_back_call(): pl.pallas_call(attend_back_kernel, grid=(m, pairs), in_specs=[pl.BlockSpe...]
    reduce_sum x32 -> x18, other arithmetic: 79.7 us -> 25.6 us  [the longest x1 9.56 us: per_device(): d_gates = jnp.stack([jnp.sum(dy * b, axis=-1) for b in branch], axis=-1)]
  transfers between devices with their start and end apart: 60 -> 29, of which waited for: 34 -> 14; matrix products, arithmetic and copies ran while one was open for 35% -> 46% of each run, Pallas kernels for 0% -> 13%
where the time goes in v1:
time: 765 us; the launch traced here: 756 us
  matrix products  221 us (29%)
  waiting for transfers between devices  145 us (19%)
  Pallas kernels  100 us (13%)
  other arithmetic  86.7 us (11%)
  local copies, waits for them, and re-layouts  76.8 us (10%)
  starting transfers between devices  72.1 us (9%)
  blocking collectives  36.5 us (5%)
  between operations  17 us (2%)
    dot_general x14, matrix products, dot(): return jnp.dot(a, b, preferred_element_type=f32)  80.6 us
    dot_general x8, matrix products, dot_nt(): lax.dot_general(a, b, (((a.ndim - 1,), (b.ndim - 1,)), ((), ())), preferr...  64.2 us
    dot_general x8, matrix products, dot_tn(): lax.dot_general(a, b, (((0,), (0,)), ((), ())), preferred_element_type=f32)  60.8 us
    all_to_all x8, waiting for transfers between devices, to_experts(): lax.all_to_all(t.reshape(all_experts, cap, D), pair, split_axis=0, concat...  59.8 us
    pallas_call x1, Pallas kernels, attend_back_call(): pl.pallas_call(attend_back_kernel, grid=(m, pairs), in_specs=[pl.BlockSpe...  46.6 us
    all_to_all x8, starting transfers between devices, to_experts(): lax.all_to_all(t.reshape(all_experts, cap, D), pair, split_axis=0, concat...  35.2 us
    pallas_call x1, Pallas kernels, attend_call(): pl.pallas_call(attend_kernel, grid=(m, pairs), in_specs=[pl.BlockSpec((1,...  29.6 us
    all_to_all x1, waiting for transfers between devices, per_device(): lax.all_to_all(jnp.broadcast_to(part_a[None], (n_dp,) + part_a.shape), 'd...  28.9 us
  transfers between devices with their start and end apart: 29, of which 14 were waited for; matrix products, arithmetic and copies ran while one was open for 46% of the time, Pallas kernels for 13%

profile of v1, /device:TPU:0, one launch (start us, length us, event | category | flops | bytes accessed | tf_op | source)
XLA Modules:
  0.0 756.3 jit_solution(765135263344514625)
XLA Ops:
  25.7 8.3 %all-reduce.3 = s32[16]{0:T(128)S(1)} all-reduce(s32[16]{0:T(128)S(1)} %bitcast_dynamic-update-slice_fusion), channel_id=2, replica_groups=mesh['dp'=4,'expert'=4,'seq'=2] {'expert','seq'}, use_global_device_ids=true, to_apply=%add.3 | all-reduce | flops 16 | bytes 128
  39.7 28.9 %all-to-all-done = bf16[4,192,1280]{2,1,0:T(8,128)(2,1)S(1)} async-done(((bf16[4,192,1280]{2,1,0:T(8,128)(2,1)}), bf16[4,192,1280]{2,1,0:T(8,128)(2,1)S(1)}, u32[]{:S(2)}, u32[]{:S(2)}) %all-to-all-start) | async-done | bytes 1966112 | tf_op jit(solution)/shard_map/all_to_all | solution.py:310
  76.4 14.3 %qkv.1 = (bf16[2,1280,1152]{2,1,0:T(8,128)(2,1)}, bf16[2,1280,768]{2,1,0:T(8,128)(2,1)}) custom-call(bf16[2,1280,768]{2,1,0:T(8,128)(2,1)} %pad_maximum_fusion.x_ref, f32[1,768]{1,0:T(1,128)} %reshape.692.gain_ref, bf16[768,1280]{1,0:T(8,128)(2,1)} %bitcast.357, f32[1280,128]{1,0:T(8,128)} %get-tuple-element.220.cos_ref, f32[1280,128]{1,0:T(8,128)} %get-tuple-element.221.sin_ref), custom_call_target="tpu_custom_call" | custom-call | tf_op jit(solution)/shard_map/qkv/pallas_call | solution.py:62
  90.7 29.6 %attend.1 = (bf16[2,1280,384]{2,1,0:T(8,128)(2,1)}, f32[2,3,2,1280]{3,2,1,0:T(2,128)}) custom-call(bf16[2,1280,1152]{2,1,0:T(8,128)(2,1)} %get-tuple-element.20.qkv_ref), custom_call_target="tpu_custom_call" | custom-call | tf_op jit(solution)/shard_map/attend/pallas_call | solution.py:125
  178.4 18.8 %all-to-all-done.3 = bf16[8,160,768]{2,1,0:T(8,128)(2,1)} async-done(((bf16[8,160,768]{2,1,0:T(8,128)(2,1)}), bf16[8,160,768]{2,1,0:T(8,128)(2,1)}, u32[]{:S(2)}, u32[]{:S(2)}) %all-to-all-start.3) | async-done | bytes 1966112 | tf_op jit(solution)/shard_map/all_to_all | solution.py:389
  208.7 10.6 %fusion.36 = f32[1280,2048]{1,0:T(8,128)} fusion(bf16[1280,768]{1,0:T(8,128)(2,1)} %bitcast.30, bf16[1,768,2048]{2,1,0:T(8,128)(2,1)} %all-gather.27.cloned.1.call-done), kind=kOutput, calls=%fused_computation.98 | convolution fusion | flops 4026531840 | bytes 15597568 | tf_op jit(solution)/shard_map/dot_general | solution.py:22
  219.2 7.7 %all-to-all-done.5 = bf16[8,160,768]{2,1,0:T(8,128)(2,1)} async-done(((bf16[8,160,768]{2,1,0:T(8,128)(2,1)}), bf16[8,160,768]{2,1,0:T(8,128)(2,1)}, u32[]{:S(2)}, u32[]{:S(2)}) %all-to-all-start.5) | async-done | bytes 1966112 | tf_op jit(solution)/shard_map/all_to_all | solution.py:389
  230.5 10.9 %fusion.44 = f32[1280,2048]{1,0:T(8,128)} fusion(bf16[1280,768]{1,0:T(8,128)(2,1)} %bitcast.30, bf16[1,768,2048]{2,1,0:T(8,128)(2,1)} %all-gather.25.cloned.1.call-done), kind=kOutput, calls=%fused_computation.106 | convolution fusion | flops 4026531840 | bytes 15597568 | tf_op jit(solution)/shard_map/dot_general | solution.py:22
  241.4 8.4 %fusion.34 = f32[1280,2048]{1,0:T(8,128)} fusion(bf16[1280,768]{1,0:T(8,128)(2,1)} %bitcast.39, bf16[1,768,2048]{2,1,0:T(8,128)(2,1)S(1)} %copy-done.65), kind=kOutput, calls=%fused_computation.96 | convolution fusion | flops 4026531840 | bytes 15597568 | tf_op jit(solution)/shard_map/dot_general | solution.py:22
  260.3 18.4 %all-gather.29.cloned.1.call-done = bf16[1,2048,768]{2,1,0:T(8,128)(2,1)} async-done(((bf16[1,512,768]{2,1,0:T(8,128)(2,1)}), bf16[1,2048,768]{2,1,0:T(8,128)(2,1)}) %all-gather.29.cloned.1.call-update) | async-done | bytes 3145744 | tf_op jit(solution)/shard_map/all_gather | solution.py:338
  278.6 18.6 %multiply_convert_fusion.2 = (bf16[1280,2048]{1,0:T(8,128)(2,1)}, bf16[1280,2048]{1,0:T(8,128)(2,1)}, bf16[1280,2048]{1,0:T(8,128)(2,1)}) fusion(f32[1280,2048]{1,0:T(8,128)} %fusion.44, f32[1280,2048]{1,0:T(8,128)} %fusion.36, bf16[1280,768]{1,0:T(8,128)(2,1)S(1)} %bitcast.386, bf16[1,2048,768]{2,1,0:T(8,128)(2,1)} %all-gather.29.cloned.1.call-done), kind=kOutput, calls=%fused_computation.5 | convolution fusion | flops 4065853440 | bytes 41811968 | tf_op jit(solution)/shard_map/dot_general | solution.py:26
  297.2 8.5 %fusion.42 = f32[1280,2048]{1,0:T(8,128)} fusion(bf16[1280,768]{1,0:T(8,128)(2,1)} %bitcast.39, bf16[1,768,2048]{2,1,0:T(8,128)(2,1)S(1)} %copy-done.68), kind=kOutput, calls=%fused_computation.104 | convolution fusion | flops 4026531840 | bytes 15597568 | tf_op jit(solution)/shard_map/dot_general | solution.py:22
  312.0 18.4 %multiply_convert_fusion = (bf16[1280,2048]{1,0:T(8,128)(2,1)}, bf16[1280,2048]{1,0:T(8,128)(2,1)}, bf16[1280,2048]{1,0:T(8,128)(2,1)}) fusion(f32[1280,2048]{1,0:T(8,128)} %fusion.42, f32[1280,2048]{1,0:T(8,128)} %fusion.34, bf16[1280,768]{1,0:T(8,128)(2,1)} %bitcast.64, bf16[1,2048,768]{2,1,0:T(8,128)(2,1)} %all-gather.29.cloned.1.call-done), kind=kOutput, calls=%fused_computation.3 | convolution fusion | flops 4065853440 | bytes 41811968 | tf_op jit(solution)/shard_map/dot_general | solution.py:26
  330.4 10.9 %add_convert_fusion = bf16[2048,768]{1,0:T(8,128)(2,1)} fusion(f32[2048,768]{1,0:T(8,128)} %fusion.108, bf16[1280,2048]{1,0:T(8,128)(2,1)} %get-tuple-element.177, bf16[1280,768]{1,0:T(8,128)(2,1)} %bitcast.64), kind=kOutput, calls=%fused_computation.17 | convolution fusion | flops 4029677568 | bytes 16646144 | tf_op jit(solution)/shard_map/dot_general | solution.py:30
  342.4 7.1 fusion.107
  349.5 7.6 %add_convert_fusion.1 = bf16[768,2048]{1,0:T(8,128)(2,1)} fusion(f32[768,2048]{1,0:T(8,128)S(1)} %fusion.107, bf16[1280,768]{1,0:T(8,128)(2,1)} %bitcast.39, bf16[1280,2048]{1,0:T(8,128)(2,1)S(1)} %bitcast.376), kind=kOutput, calls=%fused_computation.18 | convolution fusion | flops 4029677568 | bytes 16646144 | tf_op jit(solution)/shard_map/dot_general | solution.py:30
  368.3 8.0 %convolution_convert_fusion.2 = bf16[1280,768]{1,0:T(8,128)(2,1)} fusion(bf16[1280,2048]{1,0:T(8,128)(2,1)} %get-tuple-element.174, bf16[1,2048,768]{2,1,0:T(8,128)(2,1)S(1)} %copy-done.70), kind=kOutput, calls=%fused_computation.77 | convolution fusion | flops 4027514880 | bytes 10354688 | tf_op jit(solution)/shard_map/dot_general | solution.py:22
  380.8 7.3 fusion.106
  388.2 7.4 add_convert_fusion.2
  395.6 9.1 %convolution_convert_fusion.1 = bf16[1280,768]{1,0:T(8,128)(2,1)} fusion(bf16[1280,2048]{1,0:T(8,128)(2,1)} %get-tuple-element.177, bf16[1,2048,768]{2,1,0:T(8,128)(2,1)} %all-gather.29.cloned.1.call-done), kind=kOutput, calls=%fused_computation.76 | convolution fusion | flops 4027514880 | bytes 10354688 | tf_op jit(solution)/shard_map/dot_general | solution.py:22
  421.8 7.3 fusion.38
  438.2 8.9 %all-to-all-done.6 = bf16[8,160,768]{2,1,0:T(8,128)(2,1)} async-done(((bf16[8,160,768]{2,1,0:T(8,128)(2,1)}), bf16[8,160,768]{2,1,0:T(8,128)(2,1)}, u32[]{:S(2)}, u32[]{:S(2)}) %all-to-all-start.6) | async-done | bytes 1966112 | tf_op jit(solution)/shard_map/all_to_all | solution.py:389
  466.3 10.3 %all-to-all-done.8 = bf16[8,160,768]{2,1,0:T(8,128)(2,1)} async-done(((bf16[8,160,768]{2,1,0:T(8,128)(2,1)}), bf16[8,160,768]{2,1,0:T(8,128)(2,1)}, u32[]{:S(2)}, u32[]{:S(2)}) %all-to-all-start.8) | async-done | bytes 1966112 | tf_op jit(solution)/shard_map/all_to_all | solution.py:389
  481.2 9.6 %fusion.12 = (f32[1280]{0:T(1024)S(1)}, f32[1280]{0:T(1024)S(1)}, f32[1280]{0:T(1024)S(1)}, f32[1280,768]{1,0:T(8,128)}, f32[1280,768]{1,0:T(8,128)}) fusion(bf16[2,1,1,640,768]{4,3,2,1,0:T(8,128)(2,1)S(1)} %copy-done.8, f32[768]{0:T(1024)S(1)} %copy-done.39, f32[1280,768]{1,0:T(8,128)} %copy-done.2, f32[1280]{0:T(1024)S(1)} %copy-done.35, ...), kind=kLoop, calls=%fused_computation.51 | loop fusion | flops 26538240 | bytes 21707776 | tf_op jit(solution)/shard_map/reduce_sum | solution.py:432
  498.1 8.2 %all-to-all-done.10 = bf16[8,160,768]{2,1,0:T(8,128)(2,1)} async-done(((bf16[8,160,768]{2,1,0:T(8,128)(2,1)}), bf16[8,160,768]{2,1,0:T(8,128)(2,1)}, u32[]{:S(2)}, u32[]{:S(2)}) %all-to-all-start.10) | async-done | bytes 1966112 | tf_op jit(solution)/shard_map/all_to_all | solution.py:389
  562.0 46.6 %attend_back.1.low_ref = bf16[2,1280,1152]{2,1,0:T(8,128)(2,1)} custom-call(bf16[2,1280,1152]{2,1,0:T(8,128)(2,1)} %get-tuple-element.20.qkv_ref, bf16[2,1024,384]{2,1,0:T(8,128)(2,1)} %bitcast.372, bf16[2,256,384]{2,1,0:T(8,128)(2,1)} %bitcast_select_fusion.1.do_v_ref, f32[2,3,2,1280]{3,2,1,0:T(2,128)} %get-tuple-element.22.lse_ref, ...), custom_call_target="tpu_custom_call" | custom-call | tf_op jit(solution)/shard_map/attend_back/pallas_call | solution.py:176
  608.6 9.9 %din.1 = (bf16[2,1280,768]{2,1,0:T(8,128)(2,1)}, f32[1,768]{1,0:T(1,128)}) custom-call(bf16[2,1280,1152]{2,1,0:T(8,128)(2,1)} %attend_back.1.low_ref, bf16[768,1280]{1,0:T(8,128)(2,1)} %bitcast.358, bf16[2,1280,768]{2,1,0:T(8,128)(2,1)} %pad_maximum_fusion.x_ref), custom_call_target="tpu_custom_call" | custom-call | tf_op jit(solution)/shard_map/din/pallas_call | solution.py:210
  626.4 9.7 %fusion.21 = bf16[768,1152]{1,0:T(8,128)(2,1)} fusion(bf16[2,1280,768]{2,1,0:T(8,128)(2,1)} %get-tuple-element.24, bf16[2,1280,1152]{2,1,0:T(8,128)(2,1)} %attend_back.1.low_ref), kind=kOutput, calls=%fused_computation.75 | convolution fusion | flops 4530733056 | bytes 11599872 | tf_op jit(solution)/shard_map/dot_general | solution.py:30
  644.8 19.4 %all-to-all-done.13 = bf16[8,2,1,128,768]{4,3,2,1,0:T(8,128)(2,1)} async-done(((bf16[8,2,1,128,768]{4,3,2,1,0:T(8,128)(2,1)}), bf16[8,2,1,128,768]{4,3,2,1,0:T(8,128)(2,1)}, u32[]{:S(2)}, u32[]{:S(2)}) %all-to-all-start.13) | async-done | bytes 3145760 | tf_op jit(solution)/shard_map/all_to_all | solution.py:292
  670.2 15.8 %all_gather.57 = bf16[192,896]{1,0:T(8,128)(2,1)S(1)} all-gather(bf16[24,896]{1,0:T(8,128)(2,1)S(1)} %reduce_sum.352), channel_id=1, replica_groups=mesh['dp'=4,'expert'=4,'seq'=2] {'expert','seq'}, dimensions={0}, use_global_device_ids=true | all-gather | bytes 387072 | tf_op jit(solution)/shard_map/all_gather | solution.py:464
  702.2 8.1 %all-to-all-done.14 = bf16[16,48,1280]{2,1,0:T(8,128)(2,1)} async-done(((bf16[16,48,1280]{2,1,0:T(8,128)(2,1)}), bf16[16,48,1280]{2,1,0:T(8,128)(2,1)}, u32[]{:S(2)}, u32[]{:S(2)}) %all-to-all-start.14) | async-done | bytes 1966112 | tf_op jit(solution)/shard_map/all_to_all | solution.py:460
  712.1 12.4 %all-gather.5 = bf16[384,1280]{1,0:T(8,128)(2,1)S(1)} all-gather(bf16[48,1280]{1,0:T(8,128)(2,1)S(1)} %reduce_sum.345), channel_id=7, replica_groups=mesh['dp'=4,'expert'=4,'seq'=2] {'expert','seq'}, dimensions={0}, use_global_device_ids=true | all-gather | bytes 1105920 | tf_op jit(solution)/shard_map/all_gather | solution.py:478
  (451 shorter events, 314.4 us)
Async XLA Ops:
  7.2 62.3 %all-gather.23.cloned.1.call-start = ((), (), s32[]{:S(2)}) async-start(), calls=%async_computation.24 | async-start | bytes 3538944 | tf_op jit(solution)/shard_map/all_gather | solution.py:265
  9.2 63.1 %all-gather.19.cloned.1.call-start = ((), (), s32[]{:S(2)}) async-start(), calls=%async_computation.19 | async-start | bytes 4718592 | tf_op jit(solution)/shard_map/all_gather | solution.py:266
  12.0 130.7 %all-gather.21.cloned.1.call-start = ((), (), s32[]{:S(2)}) async-start(), calls=%async_computation.20 | async-start | bytes 1548288 | tf_op jit(solution)/shard_map/all_gather | solution.py:327
  16.9 51.7 %all-to-all-start = ((bf16[4,192,1280]{2,1,0:T(8,128)(2,1)}), bf16[4,192,1280]{2,1,0:T(8,128)(2,1)S(1)}, u32[]{:S(2)}, u32[]{:S(2)}) async-start(bf16[4,192,1280]{2,1,0:T(8,128)(2,1)} %broadcast_in_dim.235), calls=%async_computation | async-start | bytes 3932160 | tf_op jit(solution)/shard_map/all_to_all | solution.py:310
  23.3 185.4 %all-gather.27.cloned.1.call-start = ((), (), s32[]{:S(2)}) async-start(), calls=%async_computation.26 | async-start | bytes 3932160 | tf_op jit(solution)/shard_map/all_gather | solution.py:337
  34.9 37.3 %copy-start.52 = (pred[1,2,2,128]{3,1,2,0:T(4,128)(4,1)}, pred[1,2,2,128]{3,1,2,0:T(4,128)(4,1)S(1)}, u32[]{:S(2)}) copy-start(pred[1,2,2,128]{3,1,2,0:T(4,128)(4,1)S(1)} %copy.351) | copy-start | bytes 1540
  35.0 86.3 %copy-start.56 = (pred[2,8]{0,1:T(8,128)(4,1)}, pred[2,8]{0,1:T(8,128)(4,1)S(1)}, u32[]{:S(2)}) copy-start(pred[2,8]{0,1:T(8,128)(4,1)S(1)} %copy.273) | copy-start | bytes 52
  35.1 86.2 %copy-start.58 = (pred[2,8]{0,1:T(8,128)(4,1)}, pred[2,8]{0,1:T(8,128)(4,1)S(1)}, u32[]{:S(2)}) copy-start(pred[2,8]{0,1:T(8,128)(4,1)S(1)} %copy.274) | copy-start | bytes 52
  122.8 24.8 %all-to-all-start.2 = ((bf16[8,2,1,128,384]{4,3,2,1,0:T(8,128)(2,1)}), bf16[8,2,1,128,384]{4,3,2,1,0:T(8,128)(2,1)S(1)}, u32[]{:S(2)}, u32[]{:S(2)}) async-start(bf16[8,2,1,128,384]{4,3,2,1,0:T(8,128)(2,1)} %select_bitcast_fusion.1), calls=%async_computation.2 | async-start | bytes 3145728 | tf_op jit(solution)/shard_map/all_to_all | solution.py:292
  126.6 103.9 %all-gather.25.cloned.1.call-start = ((), (), s32[]{:S(2)}) async-start(), calls=%async_computation.25 | async-start | bytes 3932160 | tf_op jit(solution)/shard_map/all_gather | solution.py:336
  147.6 7.2 all-to-all-start.1
  167.4 29.7 %all-to-all-start.3 = ((bf16[8,160,768]{2,1,0:T(8,128)(2,1)}), bf16[8,160,768]{2,1,0:T(8,128)(2,1)}, u32[]{:S(2)}, u32[]{:S(2)}) async-start(bf16[8,160,768]{2,1,0:T(8,128)(2,1)} %bitcast.29), calls=%async_computation.3 | async-start | bytes 3932160 | tf_op jit(solution)/shard_map/all_to_all | solution.py:389
  171.9 106.7 %all-gather.29.cloned.1.call-start = ((), (), s32[]{:S(2)}) async-start(), calls=%async_computation.27 | async-start | bytes 3932160 | tf_op jit(solution)/shard_map/all_gather | solution.py:338
  197.1 29.8 %all-to-all-start.5 = ((bf16[8,160,768]{2,1,0:T(8,128)(2,1)}), bf16[8,160,768]{2,1,0:T(8,128)(2,1)}, u32[]{:S(2)}, u32[]{:S(2)}) async-start(bf16[8,160,768]{2,1,0:T(8,128)(2,1)} %bitcast.368), calls=%async_computation.5 | async-start | bytes 3932160 | tf_op jit(solution)/shard_map/all_to_all | solution.py:389
  226.9 28.8 %all-to-all-start.7 = ((bf16[8,160,768]{2,1,0:T(8,128)(2,1)}), bf16[8,160,768]{2,1,0:T(8,128)(2,1)S(1)}, u32[]{:S(2)}, u32[]{:S(2)}) async-start(bf16[8,160,768]{2,1,0:T(8,128)(2,1)} %bitcast.57), calls=%async_computation.7 | async-start | bytes 3932160 | tf_op jit(solution)/shard_map/all_to_all | solution.py:389
  255.6 56.4 %all-to-all-start.9 = ((bf16[8,160,768]{2,1,0:T(8,128)(2,1)}), bf16[8,160,768]{2,1,0:T(8,128)(2,1)}, u32[]{:S(2)}, u32[]{:S(2)}) async-start(bf16[8,160,768]{2,1,0:T(8,128)(2,1)} %bitcast.63), calls=%async_computation.9 | async-start | bytes 3932160 | tf_op jit(solution)/shard_map/all_to_all | solution.py:389
  260.0 376.1 %reduce-scatter.8.cloned.1.call-start = ((), (), s32[]{:S(2)}) async-start(), calls=%async_computation.23 | async-start | bytes 3932160 | tf_op jit(solution)/shard_map/reduce_scatter | solution.py:413
  341.4 328.8 %reduce-scatter.6.cloned.1.call-start = ((), (), s32[]{:S(2)}) async-start(), calls=%async_computation.22 | async-start | bytes 3932160 | tf_op jit(solution)/shard_map/reduce_scatter | solution.py:413
  376.3 40.5 %all-to-all-start.4 = ((bf16[8,160,768]{2,1,0:T(8,128)(2,1)}), bf16[8,160,768]{2,1,0:T(8,128)(2,1)}, u32[]{:S(2)}, u32[]{:S(2)}) async-start(bf16[8,160,768]{2,1,0:T(8,128)(2,1)} %bitcast.388), calls=%async_computation.4 | async-start | bytes 3932160 | tf_op jit(solution)/shard_map/all_to_all | solution.py:389
  380.8 316.2 %reduce-scatter.4.cloned.1.call-start = ((), (), s32[]{:S(2)}) async-start(), calls=%async_computation.21 | async-start | bytes 3932160 | tf_op jit(solution)/shard_map/reduce_scatter | solution.py:413
  416.9 30.2 %all-to-all-start.6 = ((bf16[8,160,768]{2,1,0:T(8,128)(2,1)}), bf16[8,160,768]{2,1,0:T(8,128)(2,1)}, u32[]{:S(2)}, u32[]{:S(2)}) async-start(bf16[8,160,768]{2,1,0:T(8,128)(2,1)} %bitcast.389), calls=%async_computation.6 | async-start | bytes 3932160 | tf_op jit(solution)/shard_map/all_to_all | solution.py:389
  447.0 29.6 %all-to-all-start.8 = ((bf16[8,160,768]{2,1,0:T(8,128)(2,1)}), bf16[8,160,768]{2,1,0:T(8,128)(2,1)}, u32[]{:S(2)}, u32[]{:S(2)}) async-start(bf16[8,160,768]{2,1,0:T(8,128)(2,1)} %bitcast.59), calls=%async_computation.8 | async-start | bytes 3932160 | tf_op jit(solution)/shard_map/all_to_all | solution.py:389
  476.6 29.7 %all-to-all-start.10 = ((bf16[8,160,768]{2,1,0:T(8,128)(2,1)}), bf16[8,160,768]{2,1,0:T(8,128)(2,1)}, u32[]{:S(2)}, u32[]{:S(2)}) async-start(bf16[8,160,768]{2,1,0:T(8,128)(2,1)} %bitcast.385), calls=%async_computation.10 | async-start | bytes 3932160 | tf_op jit(solution)/shard_map/all_to_all | solution.py:389
  523.1 6.2 all-to-all-start.11
  529.2 25.3 %all-to-all-start.12 = ((bf16[8,2,1,128,384]{4,3,2,1,0:T(8,128)(2,1)}), bf16[8,2,1,128,384]{4,3,2,1,0:T(8,128)(2,1)}, u32[]{:S(2)}, u32[]{:S(2)}) async-start(bf16[8,2,1,128,384]{4,3,2,1,0:T(8,128)(2,1)} %broadcast_select_fusion), calls=%async_computation.12 | async-start | bytes 3145728 | tf_op jit(solution)/shard_map/all_to_all | solution.py:470
  554.5 67.3 %all-to-all-start.15 = ((bf16[32,24,896]{2,1,0:T(8,128)(2,1)}), bf16[32,24,896]{2,1,0:T(8,128)(2,1)S(1)}, u32[]{:S(2)}, u32[]{:S(2)}) async-start(bf16[32,24,896]{2,1,0:T(8,128)(2,1)} %concatenate.101), calls=%async_computation.15 | async-start | bytes 2752512 | tf_op jit(solution)/shard_map/all_to_all | solution.py:460
  621.9 42.3 %all-to-all-start.13 = ((bf16[8,2,1,128,768]{4,3,2,1,0:T(8,128)(2,1)}), bf16[8,2,1,128,768]{4,3,2,1,0:T(8,128)(2,1)}, u32[]{:S(2)}, u32[]{:S(2)}) async-start(bf16[8,2,1,128,768]{4,3,2,1,0:T(8,128)(2,1)} %select_bitcast_fusion), calls=%async_computation.13 | async-start | bytes 6291456 | tf_op jit(solution)/shard_map/all_to_all | solution.py:292
  626.3 112.6 %all-gather.35.cloned.1.call-start = ((), (), s32[]{:S(2)}) async-start(), calls=%async_computation.30 | async-start | bytes 2359296 | tf_op jit(solution)/shard_map/all_gather | solution.py:416
  643.0 46.9 %collective-permute-start = (bf16[2,512,768]{2,1,0:T(8,128)(2,1)}, bf16[2,512,768]{2,1,0:T(8,128)(2,1)}, u32[]{:S(2)}, u32[]{:S(2)}) collective-permute-start(bf16[2,512,768]{2,1,0:T(8,128)(2,1)} %dynamic-slice_bitcast_fusion), channel_id=1, source_target_pairs={{0,1},{1,0},{2,3},{3,2},{4,5},{5,4},{6,7},{7,6},{8,9},{9,8},{10,11... | collective-permute-start | bytes 4718600 | tf_op jit(solution)/shard_map/ppermute | solution.py:487
  664.2 46.1 %all-to-all-start.14 = ((bf16[16,48,1280]{2,1,0:T(8,128)(2,1)}), bf16[16,48,1280]{2,1,0:T(8,128)(2,1)}, u32[]{:S(2)}, u32[]{:S(2)}) async-start(bf16[16,48,1280]{2,1,0:T(8,128)(2,1)} %pad_maximum_fusion.6), calls=%async_computation.14 | async-start | bytes 3932160 | tf_op jit(solution)/shard_map/all_to_all | solution.py:460
  669.4 72.9 %all-gather.33.cloned.1.call-start = ((), (), s32[]{:S(2)}) async-start(), calls=%async_computation.29 | async-start | bytes 2359296 | tf_op jit(solution)/shard_map/all_gather | solution.py:416
  670.2 75.6 %all-gather.31.cloned.1.call-start = ((), (), s32[]{:S(2)}) async-start(), calls=%async_computation.28 | async-start | bytes 2359296 | tf_op jit(solution)/shard_map/all_gather | solution.py:416
  (80 other events, 706.1 us)
Sparse Core Ops, SparseCore 0:
  10.5 34.8 all-gather.22
  47.6 12.1 all-gather.18
  61.9 25.0 all-gather.20
  88.4 63.0 all-gather.26
  153.0 62.0 all-gather.24
  216.5 62.0 all-gather.28
  341.5 59.0 reduce-scatter.7
  402.9 60.2 reduce-scatter.5
  466.1 60.3 reduce-scatter.3
  636.3 11.5 all-gather.34
  671.7 11.0 all-gather.32
  697.1 13.5 all-gather.30
